TPU v7x, 256 devices: a whole 4x4x8 slice. The times are simulated.
256 devices in a mesh: grp: 8 (over y_hi, x), blk: 32 (over z, y_lo, core).
Axes of the slice: x: 4, y: 4 (y_hi: 2, y_lo: 2; y = y_hi * 2 + y_lo), z: 8, core: 2. Of those that a mesh axis runs over, the one named last changes fastest.
Arguments:
- tokens: bfloat16 [16384, 4096], P(('blk', 'grp')), may hold values from -16 to 16
- w_query: bfloat16 [4096, 4096], P(None, 'grp'), may hold values from -0.09375 to 0.09375
- key_weight: bfloat16 [4096, 1024], P(None, 'grp'), may hold values from -0.09375 to 0.09375
- value_weight: bfloat16 [4096, 1024], P(None, 'grp'), may hold values from -0.09375 to 0.09375
- w_output: bfloat16 [4096, 4096], P('grp'), may hold values from -0.09375 to 0.09375
- block_mask: int32 [128, 128], P('blk'), may hold values from 0 to 1, as said below
- positions: int32 [16384], P('blk'), may hold values from 0 to 98301, as said below
Outputs:
- attended: bfloat16 [16384, 4096], P(('blk', 'grp'))
Inputs may be any that keep to these rules, and one draw needn't show every extreme that they name: block_mask[i, j] is 1 exactly where |i - j| <= 1, where i < 1 or j < 1, or where j is one of 3 distinct blocks drawn for row i; so query blocks below 1 attend every key block. A sequence block is a run of 512 tokens from a multiple of 512. The drawn blocks of a row never lie in its own sequence block, in the two sequence blocks beside it (the last and the first count as beside each other) or in the first sequence block. Over the query blocks of one sequence block, other than those below 1, the live key blocks that lie outside that sequence block, are not the block just before or just after it, and are not below 1, number at most 1 in any one other sequence block. positions rise along the sequence by 1 or 2 per token; the last token's position is the most.
All inputs are finite; a program needn't handle non-finite values.
Results may differ from a plain program's by a relative error of at most 0.017.
Values may be sent and summed in bfloat16 or wider, within the bound.
A program may use at most 64 MiB of HBM per device.

v0:
```python
import jax
import jax.numpy as jnp
from jax import lax
from jax.sharding import PartitionSpec as P

HEAD_WIDTH = 128
MASK_BLOCK_TOKENS = 128


NEG_FILL = -1e30


def rotary_position(projected, positions, heads):
    half = HEAD_WIDTH // 2
    inverse = jnp.power(
        jnp.float32(500000.0), -(2.0 * jnp.arange(half, dtype=jnp.float32)) / HEAD_WIDTH
    )
    angles = positions.astype(jnp.float32)[:, None] * inverse[None, :]
    cosine = jnp.cos(angles)[:, None, :]
    sine = jnp.sin(angles)[:, None, :]
    shaped = projected.reshape(projected.shape[0], heads, HEAD_WIDTH)
    first = shaped[..., :half]
    second = shaped[..., half:]
    turned = jnp.concatenate(
        [first * cosine - second * sine, second * cosine + first * sine], axis=-1
    )
    return turned.reshape(projected.shape[0], heads * HEAD_WIDTH)


def attend(state, query_tile, key_tile, value_tile, column_live):
    top_old, total_old, accum_old = state
    scores = jnp.einsum(
        "crd,gcd->crg", query_tile, key_tile, preferred_element_type=jnp.float32
    ) * HEAD_WIDTH ** (-0.5)
    scores = jnp.where(column_live[None, None, :], scores, NEG_FILL)
    top_new = jnp.maximum(top_old, jnp.max(scores, axis=-1))
    weights = jnp.where(column_live[None, None, :], jnp.exp(scores - top_new[..., None]), 0.0)
    factor = jnp.exp(top_old - top_new)
    total_new = total_old * factor + jnp.sum(weights, axis=-1)
    product = jnp.einsum(
        "crg,gcd->crd", weights.astype(jnp.bfloat16), value_tile, preferred_element_type=jnp.float32
    )
    return (top_new, total_new, accum_old * factor[..., None] + product)


def fold_tiles(fold_state, query_tiles, key_tile, value_tile, live_cols):

    def over_query(unused, query_items):
        query_tile, top_old, total_old, accum_old, live_blocks = query_items
        column_live = jnp.repeat(live_blocks, MASK_BLOCK_TOKENS)
        updated = lax.cond(
            jnp.any(live_blocks),
            lambda: attend(
                (top_old, total_old, accum_old), query_tile, key_tile, value_tile, column_live
            ),
            lambda: (top_old, total_old, accum_old),
        )
        return (unused, updated)

    unused, new_state = lax.scan(
        over_query, 0, (query_tiles, fold_state[0], fold_state[1], fold_state[2], live_cols)
    )
    return new_state


def body(tokens, w_query, key_weight, value_weight, w_output, block_mask, positions):
    query_cols = w_query.shape[1]
    key_cols = key_weight.shape[1]
    query_heads = query_cols // HEAD_WIDTH
    kv_heads = key_cols // HEAD_WIDTH
    head_repeat_count = query_heads // kv_heads
    tile_rows = head_repeat_count * MASK_BLOCK_TOKENS
    piece = lax.all_gather(tokens, "grp", axis=0, tiled=True)
    projected = jnp.concatenate(
        [
            jnp.dot(piece, w_query, preferred_element_type=jnp.float32),
            jnp.dot(piece, key_weight, preferred_element_type=jnp.float32),
            jnp.dot(piece, value_weight, preferred_element_type=jnp.float32),
        ],
        axis=1,
    )
    block_rows = projected.shape[0]
    query_rows = rotary_position(projected[:, :query_cols], positions, query_heads).astype(
        jnp.bfloat16
    )
    key_rows = rotary_position(
        projected[:, query_cols : query_cols + key_cols], positions, kv_heads
    ).astype(jnp.bfloat16)
    value_rows = projected[:, query_cols + key_cols :].astype(jnp.bfloat16)
    query_block_rows = block_rows // MASK_BLOCK_TOKENS
    query_tiles = query_rows.reshape(
        query_block_rows, MASK_BLOCK_TOKENS, kv_heads, head_repeat_count, HEAD_WIDTH
    )
    query_tiles = query_tiles.transpose(0, 2, 3, 1, 4).reshape(
        query_block_rows, kv_heads, tile_rows, HEAD_WIDTH
    )
    live_rows = block_mask != 0
    initial = (
        jnp.full((query_block_rows, kv_heads, tile_rows), NEG_FILL, jnp.float32),
        jnp.zeros((query_block_rows, kv_heads, tile_rows), jnp.float32),
        jnp.zeros((query_block_rows, kv_heads, tile_rows, HEAD_WIDTH), jnp.float32),
    )
    key_piece = lax.all_gather(key_rows, "blk", axis=0, tiled=True)
    value_piece = lax.all_gather(value_rows, "blk", axis=0, tiled=True)
    piece_rows = key_piece.shape[0]
    group_count = piece_rows // block_rows
    key_groups = key_piece.reshape(group_count, block_rows, kv_heads, HEAD_WIDTH)
    value_groups = value_piece.reshape(group_count, block_rows, kv_heads, HEAD_WIDTH)

    def over_group(fold_state, group_items):
        key_tile, value_tile, group_index = group_items
        first_key_block = group_index * block_rows // MASK_BLOCK_TOKENS
        live_cols = lax.dynamic_slice(
            live_rows,
            (jnp.int32(0), first_key_block),
            (query_block_rows, block_rows // MASK_BLOCK_TOKENS),
        )
        return (fold_tiles(fold_state, query_tiles, key_tile, value_tile, live_cols), 0)

    result, unused = lax.scan(
        over_group, initial, (key_groups, value_groups, jnp.arange(group_count))
    )
    top_all, total_all, accum_all = result
    safe_total = jnp.where(total_all > 0, total_all, 1.0)
    mixed_tiles = accum_all / safe_total[..., None]
    mixed = mixed_tiles.reshape(
        query_block_rows, kv_heads, head_repeat_count, MASK_BLOCK_TOKENS, HEAD_WIDTH
    )
    mixed = mixed.transpose(0, 3, 1, 2, 4).reshape(block_rows, query_cols).astype(jnp.bfloat16)
    term = jnp.dot(mixed, w_output, preferred_element_type=jnp.float32)
    return lax.psum_scatter(
        lax.optimization_barrier(term.astype(jnp.bfloat16))
        .astype(jnp.float32)
        .astype(jnp.bfloat16),
        "grp",
        scatter_dimension=0,
        tiled=True,
    )


def solution(mesh):
    return jax.shard_map(
        body,
        mesh=mesh,
        in_specs=(
            P(("blk", "grp"), None),
            P(None, "grp"),
            P(None, "grp"),
            P(None, "grp"),
            P("grp", None),
            P("blk", None),
            P("blk"),
        ),
        out_specs=P(("blk", "grp"), None),
        check_vma=False,
    )
```

profile of v0, /device:TPU:2, one launch (start us, length us, event | category | flops | bytes accessed | tf_op | source)
XLA Modules:
  0.0 990.6 jit_solution(6580860775781006994)
XLA Ops:
  8.0 80.4 %all-gather.5.cloned.1.call-done = bf16[512,4096]{1,0:T(8,128)(2,1)} async-done(((bf16[64,4096]{1,0:T(8,128)(2,1)}), bf16[512,4096]{1,0:T(8,128)(2,1)}) %all-gather.5.cloned.1.call-update) | async-done | bytes 4194320 | tf_op jit(solution)/shard_map/all_gather | solution.py:73
  93.5 4.1 convolution_convert_fusion.1
  98.2 5.8 fusion.27
  104.8 54.5 %all-gather.9.cloned.1.call-done = bf16[16384,1,128]{0,2,1:T(8,128)(2,1)} async-done(((bf16[512,1,128]{0,2,1:T(8,128)(2,1)}), bf16[16384,1,128]{0,2,1:T(8,128)(2,1)}) %all-gather.9.cloned.1.call-update) | async-done | bytes 4194320 | tf_op jit(solution)/shard_map/all_gather | solution.py:103
  159.2 6.4 copy.15
  165.7 61.7 %all-gather.7.cloned.1.call-done = bf16[16384,128]{1,0:T(8,128)(2,1)} async-done(((bf16[512,128]{1,0:T(8,128)(2,1)}), bf16[16384,128]{1,0:T(8,128)(2,1)}) %all-gather.7.cloned.1.call-update) | async-done | bytes 4194320 | tf_op jit(solution)/shard_map/all_gather | solution.py:104
  227.4 662.9 %while.41 = (s32[]{:T(128)}, f32[4,1,512]{2,1,0:T(1,128)S(1)}, f32[4,1,512]{2,1,0:T(1,128)S(1)}, f32[4,1,512,128]{3,2,1,0:T(8,128)S(1)}, s32[32]{0:T(128)S(1)}, ...) while((s32[]{:T(128)}, f32[4,1,512]{2,1,0:T(1,128)S(1)}, ...), condition=%wide.region_8.9_spmd, body=%wide.region_0.8_spmd.sunk | while | flops 136709136 | bytes 5688032 | solution.py:120
  229.8 28.3 %while.42 = (s32[]{:T(128)}, f32[4,1,512]{2,1,0:T(1,128)S(1)}, f32[4,1,512]{2,1,0:T(1,128)S(1)}, f32[4,1,512,128]{3,2,1,0:T(8,128)S(1)}, pred[4,4]{1,0:T(4,128)(...) while((s32[]{:T(128)}, f32[4,1,512]{2,1,0:T(1,128)S(1)}, ...), condition=%wide.region_7.7_spmd.clone, body=%wide.region_1.6_spmd.clone.sunk | while | flops 136709120 | bytes 5163259 | solution.py:60
  260.4 20.7 %while.42 = (s32[]{:T(128)}, f32[4,1,512]{2,1,0:T(1,128)S(1)}, f32[4,1,512]{2,1,0:T(1,128)S(1)}, f32[4,1,512,128]{3,2,1,0:T(8,128)S(1)}, pred[4,4]{1,0:T(4,128)(...) while((s32[]{:T(128)}, f32[4,1,512]{2,1,0:T(1,128)S(1)}, ...), condition=%wide.region_7.7_spmd.clone, body=%wide.region_1.6_spmd.clone.sunk | while | flops 136709120 | bytes 5163259 | solution.py:60
  283.4 20.7 %while.42 = (s32[]{:T(128)}, f32[4,1,512]{2,1,0:T(1,128)S(1)}, f32[4,1,512]{2,1,0:T(1,128)S(1)}, f32[4,1,512,128]{3,2,1,0:T(8,128)S(1)}, pred[4,4]{1,0:T(4,128)(...) while((s32[]{:T(128)}, f32[4,1,512]{2,1,0:T(1,128)S(1)}, ...), condition=%wide.region_7.7_spmd.clone, body=%wide.region_1.6_spmd.clone.sunk | while | flops 136709120 | bytes 5163259 | solution.py:60
  306.4 16.8 %while.42 = (s32[]{:T(128)}, f32[4,1,512]{2,1,0:T(1,128)S(1)}, f32[4,1,512]{2,1,0:T(1,128)S(1)}, f32[4,1,512,128]{3,2,1,0:T(8,128)S(1)}, pred[4,4]{1,0:T(4,128)(...) while((s32[]{:T(128)}, f32[4,1,512]{2,1,0:T(1,128)S(1)}, ...), condition=%wide.region_7.7_spmd.clone, body=%wide.region_1.6_spmd.clone.sunk | while | flops 136709120 | bytes 5163259 | solution.py:60
  325.6 16.8 %while.42 = (s32[]{:T(128)}, f32[4,1,512]{2,1,0:T(1,128)S(1)}, f32[4,1,512]{2,1,0:T(1,128)S(1)}, f32[4,1,512,128]{3,2,1,0:T(8,128)S(1)}, pred[4,4]{1,0:T(4,128)(...) while((s32[]{:T(128)}, f32[4,1,512]{2,1,0:T(1,128)S(1)}, ...), condition=%wide.region_7.7_spmd.clone, body=%wide.region_1.6_spmd.clone.sunk | while | flops 136709120 | bytes 5163259 | solution.py:60
  344.7 16.8 %while.42 = (s32[]{:T(128)}, f32[4,1,512]{2,1,0:T(1,128)S(1)}, f32[4,1,512]{2,1,0:T(1,128)S(1)}, f32[4,1,512,128]{3,2,1,0:T(8,128)S(1)}, pred[4,4]{1,0:T(4,128)(...) while((s32[]{:T(128)}, f32[4,1,512]{2,1,0:T(1,128)S(1)}, ...), condition=%wide.region_7.7_spmd.clone, body=%wide.region_1.6_spmd.clone.sunk | while | flops 136709120 | bytes 5163259 | solution.py:60
  347.2 3.9 conditional.3
  363.9 20.7 %while.42 = (s32[]{:T(128)}, f32[4,1,512]{2,1,0:T(1,128)S(1)}, f32[4,1,512]{2,1,0:T(1,128)S(1)}, f32[4,1,512,128]{3,2,1,0:T(8,128)S(1)}, pred[4,4]{1,0:T(4,128)(...) while((s32[]{:T(128)}, f32[4,1,512]{2,1,0:T(1,128)S(1)}, ...), condition=%wide.region_7.7_spmd.clone, body=%wide.region_1.6_spmd.clone.sunk | while | flops 136709120 | bytes 5163259 | solution.py:60
  366.4 3.9 conditional.3
  386.9 20.7 %while.42 = (s32[]{:T(128)}, f32[4,1,512]{2,1,0:T(1,128)S(1)}, f32[4,1,512]{2,1,0:T(1,128)S(1)}, f32[4,1,512,128]{3,2,1,0:T(8,128)S(1)}, pred[4,4]{1,0:T(4,128)(...) while((s32[]{:T(128)}, f32[4,1,512]{2,1,0:T(1,128)S(1)}, ...), condition=%wide.region_7.7_spmd.clone, body=%wide.region_1.6_spmd.clone.sunk | while | flops 136709120 | bytes 5163259 | solution.py:60
  409.9 20.7 %while.42 = (s32[]{:T(128)}, f32[4,1,512]{2,1,0:T(1,128)S(1)}, f32[4,1,512]{2,1,0:T(1,128)S(1)}, f32[4,1,512,128]{3,2,1,0:T(8,128)S(1)}, pred[4,4]{1,0:T(4,128)(...) while((s32[]{:T(128)}, f32[4,1,512]{2,1,0:T(1,128)S(1)}, ...), condition=%wide.region_7.7_spmd.clone, body=%wide.region_1.6_spmd.clone.sunk | while | flops 136709120 | bytes 5163259 | solution.py:60
  432.9 20.7 %while.42 = (s32[]{:T(128)}, f32[4,1,512]{2,1,0:T(1,128)S(1)}, f32[4,1,512]{2,1,0:T(1,128)S(1)}, f32[4,1,512,128]{3,2,1,0:T(8,128)S(1)}, pred[4,4]{1,0:T(4,128)(...) while((s32[]{:T(128)}, f32[4,1,512]{2,1,0:T(1,128)S(1)}, ...), condition=%wide.region_7.7_spmd.clone, body=%wide.region_1.6_spmd.clone.sunk | while | flops 136709120 | bytes 5163259 | solution.py:60
  455.9 16.8 %while.42 = (s32[]{:T(128)}, f32[4,1,512]{2,1,0:T(1,128)S(1)}, f32[4,1,512]{2,1,0:T(1,128)S(1)}, f32[4,1,512,128]{3,2,1,0:T(8,128)S(1)}, pred[4,4]{1,0:T(4,128)(...) while((s32[]{:T(128)}, f32[4,1,512]{2,1,0:T(1,128)S(1)}, ...), condition=%wide.region_7.7_spmd.clone, body=%wide.region_1.6_spmd.clone.sunk | while | flops 136709120 | bytes 5163259 | solution.py:60
  475.0 16.8 %while.42 = (s32[]{:T(128)}, f32[4,1,512]{2,1,0:T(1,128)S(1)}, f32[4,1,512]{2,1,0:T(1,128)S(1)}, f32[4,1,512,128]{3,2,1,0:T(8,128)S(1)}, pred[4,4]{1,0:T(4,128)(...) while((s32[]{:T(128)}, f32[4,1,512]{2,1,0:T(1,128)S(1)}, ...), condition=%wide.region_7.7_spmd.clone, body=%wide.region_1.6_spmd.clone.sunk | while | flops 136709120 | bytes 5163259 | solution.py:60
  494.2 16.8 %while.42 = (s32[]{:T(128)}, f32[4,1,512]{2,1,0:T(1,128)S(1)}, f32[4,1,512]{2,1,0:T(1,128)S(1)}, f32[4,1,512,128]{3,2,1,0:T(8,128)S(1)}, pred[4,4]{1,0:T(4,128)(...) while((s32[]{:T(128)}, f32[4,1,512]{2,1,0:T(1,128)S(1)}, ...), condition=%wide.region_7.7_spmd.clone, body=%wide.region_1.6_spmd.clone.sunk | while | flops 136709120 | bytes 5163259 | solution.py:60
  496.7 3.9 conditional.3
  513.3 16.8 %while.42 = (s32[]{:T(128)}, f32[4,1,512]{2,1,0:T(1,128)S(1)}, f32[4,1,512]{2,1,0:T(1,128)S(1)}, f32[4,1,512,128]{3,2,1,0:T(8,128)S(1)}, pred[4,4]{1,0:T(4,128)(...) while((s32[]{:T(128)}, f32[4,1,512]{2,1,0:T(1,128)S(1)}, ...), condition=%wide.region_7.7_spmd.clone, body=%wide.region_1.6_spmd.clone.sunk | while | flops 136709120 | bytes 5163259 | solution.py:60
  515.8 3.9 conditional.3
  532.5 20.7 %while.42 = (s32[]{:T(128)}, f32[4,1,512]{2,1,0:T(1,128)S(1)}, f32[4,1,512]{2,1,0:T(1,128)S(1)}, f32[4,1,512,128]{3,2,1,0:T(8,128)S(1)}, pred[4,4]{1,0:T(4,128)(...) while((s32[]{:T(128)}, f32[4,1,512]{2,1,0:T(1,128)S(1)}, ...), condition=%wide.region_7.7_spmd.clone, body=%wide.region_1.6_spmd.clone.sunk | while | flops 136709120 | bytes 5163259 | solution.py:60
  555.5 20.7 %while.42 = (s32[]{:T(128)}, f32[4,1,512]{2,1,0:T(1,128)S(1)}, f32[4,1,512]{2,1,0:T(1,128)S(1)}, f32[4,1,512,128]{3,2,1,0:T(8,128)S(1)}, pred[4,4]{1,0:T(4,128)(...) while((s32[]{:T(128)}, f32[4,1,512]{2,1,0:T(1,128)S(1)}, ...), condition=%wide.region_7.7_spmd.clone, body=%wide.region_1.6_spmd.clone.sunk | while | flops 136709120 | bytes 5163259 | solution.py:60
  578.5 16.8 %while.42 = (s32[]{:T(128)}, f32[4,1,512]{2,1,0:T(1,128)S(1)}, f32[4,1,512]{2,1,0:T(1,128)S(1)}, f32[4,1,512,128]{3,2,1,0:T(8,128)S(1)}, pred[4,4]{1,0:T(4,128)(...) while((s32[]{:T(128)}, f32[4,1,512]{2,1,0:T(1,128)S(1)}, ...), condition=%wide.region_7.7_spmd.clone, body=%wide.region_1.6_spmd.clone.sunk | while | flops 136709120 | bytes 5163259 | solution.py:60
  597.6 16.8 %while.42 = (s32[]{:T(128)}, f32[4,1,512]{2,1,0:T(1,128)S(1)}, f32[4,1,512]{2,1,0:T(1,128)S(1)}, f32[4,1,512,128]{3,2,1,0:T(8,128)S(1)}, pred[4,4]{1,0:T(4,128)(...) while((s32[]{:T(128)}, f32[4,1,512]{2,1,0:T(1,128)S(1)}, ...), condition=%wide.region_7.7_spmd.clone, body=%wide.region_1.6_spmd.clone.sunk | while | flops 136709120 | bytes 5163259 | solution.py:60
  616.8 16.8 %while.42 = (s32[]{:T(128)}, f32[4,1,512]{2,1,0:T(1,128)S(1)}, f32[4,1,512]{2,1,0:T(1,128)S(1)}, f32[4,1,512,128]{3,2,1,0:T(8,128)S(1)}, pred[4,4]{1,0:T(4,128)(...) while((s32[]{:T(128)}, f32[4,1,512]{2,1,0:T(1,128)S(1)}, ...), condition=%wide.region_7.7_spmd.clone, body=%wide.region_1.6_spmd.clone.sunk | while | flops 136709120 | bytes 5163259 | solution.py:60
  635.9 16.8 %while.42 = (s32[]{:T(128)}, f32[4,1,512]{2,1,0:T(1,128)S(1)}, f32[4,1,512]{2,1,0:T(1,128)S(1)}, f32[4,1,512,128]{3,2,1,0:T(8,128)S(1)}, pred[4,4]{1,0:T(4,128)(...) while((s32[]{:T(128)}, f32[4,1,512]{2,1,0:T(1,128)S(1)}, ...), condition=%wide.region_7.7_spmd.clone, body=%wide.region_1.6_spmd.clone.sunk | while | flops 136709120 | bytes 5163259 | solution.py:60
  638.4 3.9 conditional.3
  655.1 16.8 %while.42 = (s32[]{:T(128)}, f32[4,1,512]{2,1,0:T(1,128)S(1)}, f32[4,1,512]{2,1,0:T(1,128)S(1)}, f32[4,1,512,128]{3,2,1,0:T(8,128)S(1)}, pred[4,4]{1,0:T(4,128)(...) while((s32[]{:T(128)}, f32[4,1,512]{2,1,0:T(1,128)S(1)}, ...), condition=%wide.region_7.7_spmd.clone, body=%wide.region_1.6_spmd.clone.sunk | while | flops 136709120 | bytes 5163259 | solution.py:60
  674.3 16.8 %while.42 = (s32[]{:T(128)}, f32[4,1,512]{2,1,0:T(1,128)S(1)}, f32[4,1,512]{2,1,0:T(1,128)S(1)}, f32[4,1,512,128]{3,2,1,0:T(8,128)S(1)}, pred[4,4]{1,0:T(4,128)(...) while((s32[]{:T(128)}, f32[4,1,512]{2,1,0:T(1,128)S(1)}, ...), condition=%wide.region_7.7_spmd.clone, body=%wide.region_1.6_spmd.clone.sunk | while | flops 136709120 | bytes 5163259 | solution.py:60
  693.4 16.8 %while.42 = (s32[]{:T(128)}, f32[4,1,512]{2,1,0:T(1,128)S(1)}, f32[4,1,512]{2,1,0:T(1,128)S(1)}, f32[4,1,512,128]{3,2,1,0:T(8,128)S(1)}, pred[4,4]{1,0:T(4,128)(...) while((s32[]{:T(128)}, f32[4,1,512]{2,1,0:T(1,128)S(1)}, ...), condition=%wide.region_7.7_spmd.clone, body=%wide.region_1.6_spmd.clone.sunk | while | flops 136709120 | bytes 5163259 | solution.py:60
  712.6 16.8 %while.42 = (s32[]{:T(128)}, f32[4,1,512]{2,1,0:T(1,128)S(1)}, f32[4,1,512]{2,1,0:T(1,128)S(1)}, f32[4,1,512,128]{3,2,1,0:T(8,128)S(1)}, pred[4,4]{1,0:T(4,128)(...) while((s32[]{:T(128)}, f32[4,1,512]{2,1,0:T(1,128)S(1)}, ...), condition=%wide.region_7.7_spmd.clone, body=%wide.region_1.6_spmd.clone.sunk | while | flops 136709120 | bytes 5163259 | solution.py:60
  715.1 3.9 conditional.3
  731.7 20.7 %while.42 = (s32[]{:T(128)}, f32[4,1,512]{2,1,0:T(1,128)S(1)}, f32[4,1,512]{2,1,0:T(1,128)S(1)}, f32[4,1,512,128]{3,2,1,0:T(8,128)S(1)}, pred[4,4]{1,0:T(4,128)(...) while((s32[]{:T(128)}, f32[4,1,512]{2,1,0:T(1,128)S(1)}, ...), condition=%wide.region_7.7_spmd.clone, body=%wide.region_1.6_spmd.clone.sunk | while | flops 136709120 | bytes 5163259 | solution.py:60
  754.7 16.8 %while.42 = (s32[]{:T(128)}, f32[4,1,512]{2,1,0:T(1,128)S(1)}, f32[4,1,512]{2,1,0:T(1,128)S(1)}, f32[4,1,512,128]{3,2,1,0:T(8,128)S(1)}, pred[4,4]{1,0:T(4,128)(...) while((s32[]{:T(128)}, f32[4,1,512]{2,1,0:T(1,128)S(1)}, ...), condition=%wide.region_7.7_spmd.clone, body=%wide.region_1.6_spmd.clone.sunk | while | flops 136709120 | bytes 5163259 | solution.py:60
  773.9 16.8 %while.42 = (s32[]{:T(128)}, f32[4,1,512]{2,1,0:T(1,128)S(1)}, f32[4,1,512]{2,1,0:T(1,128)S(1)}, f32[4,1,512,128]{3,2,1,0:T(8,128)S(1)}, pred[4,4]{1,0:T(4,128)(...) while((s32[]{:T(128)}, f32[4,1,512]{2,1,0:T(1,128)S(1)}, ...), condition=%wide.region_7.7_spmd.clone, body=%wide.region_1.6_spmd.clone.sunk | while | flops 136709120 | bytes 5163259 | solution.py:60
  793.0 16.8 %while.42 = (s32[]{:T(128)}, f32[4,1,512]{2,1,0:T(1,128)S(1)}, f32[4,1,512]{2,1,0:T(1,128)S(1)}, f32[4,1,512,128]{3,2,1,0:T(8,128)S(1)}, pred[4,4]{1,0:T(4,128)(...) while((s32[]{:T(128)}, f32[4,1,512]{2,1,0:T(1,128)S(1)}, ...), condition=%wide.region_7.7_spmd.clone, body=%wide.region_1.6_spmd.clone.sunk | while | flops 136709120 | bytes 5163259 | solution.py:60
  795.5 3.9 conditional.3
  812.2 20.7 %while.42 = (s32[]{:T(128)}, f32[4,1,512]{2,1,0:T(1,128)S(1)}, f32[4,1,512]{2,1,0:T(1,128)S(1)}, f32[4,1,512,128]{3,2,1,0:T(8,128)S(1)}, pred[4,4]{1,0:T(4,128)(...) while((s32[]{:T(128)}, f32[4,1,512]{2,1,0:T(1,128)S(1)}, ...), condition=%wide.region_7.7_spmd.clone, body=%wide.region_1.6_spmd.clone.sunk | while | flops 136709120 | bytes 5163259 | solution.py:60
  835.2 16.8 %while.42 = (s32[]{:T(128)}, f32[4,1,512]{2,1,0:T(1,128)S(1)}, f32[4,1,512]{2,1,0:T(1,128)S(1)}, f32[4,1,512,128]{3,2,1,0:T(8,128)S(1)}, pred[4,4]{1,0:T(4,128)(...) while((s32[]{:T(128)}, f32[4,1,512]{2,1,0:T(1,128)S(1)}, ...), condition=%wide.region_7.7_spmd.clone, body=%wide.region_1.6_spmd.clone.sunk | while | flops 136709120 | bytes 5163259 | solution.py:60
  854.3 16.8 %while.42 = (s32[]{:T(128)}, f32[4,1,512]{2,1,0:T(1,128)S(1)}, f32[4,1,512]{2,1,0:T(1,128)S(1)}, f32[4,1,512,128]{3,2,1,0:T(8,128)S(1)}, pred[4,4]{1,0:T(4,128)(...) while((s32[]{:T(128)}, f32[4,1,512]{2,1,0:T(1,128)S(1)}, ...), condition=%wide.region_7.7_spmd.clone, body=%wide.region_1.6_spmd.clone.sunk | while | flops 136709120 | bytes 5163259 | solution.py:60
  873.5 16.8 %while.42 = (s32[]{:T(128)}, f32[4,1,512]{2,1,0:T(1,128)S(1)}, f32[4,1,512]{2,1,0:T(1,128)S(1)}, f32[4,1,512,128]{3,2,1,0:T(8,128)S(1)}, pred[4,4]{1,0:T(4,128)(...) while((s32[]{:T(128)}, f32[4,1,512]{2,1,0:T(1,128)S(1)}, ...), condition=%wide.region_7.7_spmd.clone, body=%wide.region_1.6_spmd.clone.sunk | while | flops 136709120 | bytes 5163259 | solution.py:60
  891.1 6.5 convolution_convert_fusion
  897.7 86.4 %reduce-scatter.2.cloned.1.call-done = bf16[64,4096]{1,0:T(8,128)(2,1)} async-done(((bf16[512,4096]{1,0:T(8,128)(2,1)}), bf16[64,4096]{1,0:T(8,128)(2,1)}) %reduce-scatter.2.cloned.1.call-update) | async-done | bytes 524304 | tf_op jit(solution)/shard_map/reduce_scatter | solution.py:131
  (1416 shorter events, 718.6 us)
Async XLA Ops:
  6.5 81.9 %copy-start = (bf16[4096,128]{1,0:T(8,128)(2,1)S(1)}, bf16[4096,128]{1,0:T(8,128)(2,1)}, u32[]{:S(2)}) copy-start(bf16[4096,128]{1,0:T(8,128)(2,1)} %param.15) | copy-start | bytes 3145732
  6.5 81.9 %all-gather.5.cloned.1.call-start = ((), (), s32[]{:S(2)}) async-start(), calls=%async_computation.1 | async-start | bytes 4718592 | tf_op jit(solution)/shard_map/all_gather | solution.py:73
  7.3 152.0 %all-gather.9.cloned.1.call-start = ((), (), s32[]{:S(2)}) async-start(), calls=%async_computation.4 | async-start | bytes 4325376 | tf_op jit(solution)/shard_map/all_gather | solution.py:103
  8.0 85.4 %copy-start.2 = (bf16[4096,128]{1,0:T(8,128)(2,1)S(1)}, bf16[4096,128]{1,0:T(8,128)(2,1)}, u32[]{:S(2)}) copy-start(bf16[4096,128]{1,0:T(8,128)(2,1)} %param.16) | copy-start | bytes 3145732
  92.1 5.5 copy-start.1
  93.4 133.9 %all-gather.7.cloned.1.call-start = ((), (), s32[]{:S(2)}) async-start(), calls=%async_computation.2 | async-start | bytes 4325376 | tf_op jit(solution)/shard_map/all_gather | solution.py:104
  97.6 886.5 %reduce-scatter.2.cloned.1.call-start = ((), (), s32[]{:S(2)}) async-start(), calls=%async_computation.3 | async-start | bytes 4718592 | tf_op jit(solution)/shard_map/reduce_scatter | solution.py:131
Sparse Core Ops, SparseCore 0:
  10.0 78.4 all-gather.4
  93.5 65.6 all-gather.8
  161.1 66.1 all-gather.6
  897.8 86.2 reduce-scatter.1
where the time goes:
time: 1000 us; the launch traced here: 991 us
  local copies, waits for them, and re-layouts  321 us (32%)
  waiting for transfers between devices  284 us (28%)
  other arithmetic  182 us (18%)
  loops' own time  99.9 us (10%)
  matrix products  91.2 us (9%)
  between operations  13.3 us (1%)
    dynamic_update_slice x384, local copies, waits for them, and re-layouts, fold_tiles(): lax.scan(over_query, 0, (query_tiles, fold_state[0], fold_state[1], fold_...  93.6 us
    while x128, local copies, waits for them, and re-layouts  87.2 us
    reduce_scatter x1, waiting for transfers between devices, body(): lax.psum_scatter(lax.optimization_barrier(term.astype(jnp.bfloat16)).asty...  86.4 us
    reduce_or x128, other arithmetic, over_query(): jnp.any(live_blocks)  80.6 us
    all_gather x1, waiting for transfers between devices, body(): piece = lax.all_gather(tokens, 'grp', axis=0, tiled=True)  80.4 us
    squeeze x256, local copies, waits for them, and re-layouts, fold_tiles(): lax.scan(over_query, 0, (query_tiles, fold_state[0], fold_state[1], fold_...  76.6 us
    another operation x32, loops' own time, fold_tiles(): lax.scan(over_query, 0, (query_tiles, fold_state[0], fold_state[1], fold_...  76.5 us
    all_gather x1, waiting for transfers between devices, body(): value_piece = lax.all_gather(value_rows, 'blk', axis=0, tiled=True)  61.7 us
  transfers between devices with their start and end apart: 4, of which 4 were waited for; matrix products, arithmetic and copies ran while one was open for 2% of the time, Pallas kernels for 0%

commit v1 on v0

v1 whole, which is shorter than its diff:
```python
import functools

import jax
import jax.numpy as jnp
from jax import lax
from jax.experimental import pallas as pl
from jax.experimental.pallas import tpu as pltpu
from jax.sharding import PartitionSpec as P

HEAD = 128
BLOCK = 128
NEG = -1e30
LOG2E = 1.4426950408889634
SCALE2 = HEAD ** (-0.5) * LOG2E


def rotary_tables(positions):
    half = HEAD // 2
    inverse = jnp.power(
        jnp.float32(500000.0), -(2.0 * jnp.arange(half, dtype=jnp.float32)) / HEAD
    )
    angles = positions.astype(jnp.float32)[:, None] * inverse[None, :]
    cosine, sine = jnp.cos(angles), jnp.sin(angles)
    return (
        jnp.concatenate([cosine, cosine], axis=1),
        jnp.concatenate([-sine, sine], axis=1),
    )


def turn(v, cosine, sine):
    return v * cosine + pltpu.roll(v, HEAD // 2, 1) * sine


def project_kernel(x_ref, wq_ref, wk_ref, wv_ref, cos_ref, sin_ref, q_ref, kv_ref):
    cosine, sine = cos_ref[...], sin_ref[...]
    x = x_ref[...]
    k = jnp.dot(x, wk_ref[...], preferred_element_type=jnp.float32)
    kv_ref[:, :HEAD] = turn(k, cosine, sine).astype(jnp.bfloat16)
    v = jnp.dot(x, wv_ref[...], preferred_element_type=jnp.float32)
    kv_ref[:, HEAD:] = v.astype(jnp.bfloat16)
    q = jnp.dot(x, wq_ref[...], preferred_element_type=jnp.float32)
    for h in range(wq_ref.shape[1] // HEAD):
        cols = slice(h * HEAD, (h + 1) * HEAD)
        q_ref[:, cols] = turn(q[:, cols], cosine, sine).astype(jnp.bfloat16)


def project(piece, wq, wk, wv, cosine, sine):
    rows = piece.shape[0]
    step = 128
    return pl.pallas_call(
        project_kernel,
        grid=(rows // step,),
        in_specs=[
            pl.BlockSpec((step, piece.shape[1]), lambda i: (i, 0)),
            pl.BlockSpec(wq.shape, lambda i: (0, 0)),
            pl.BlockSpec(wk.shape, lambda i: (0, 0)),
            pl.BlockSpec(wv.shape, lambda i: (0, 0)),
            pl.BlockSpec((step, HEAD), lambda i: (i, 0)),
            pl.BlockSpec((step, HEAD), lambda i: (i, 0)),
        ],
        out_specs=[
            pl.BlockSpec((step, wq.shape[1]), lambda i: (i, 0)),
            pl.BlockSpec((step, 2 * HEAD), lambda i: (i, 0)),
        ],
        out_shape=[
            jax.ShapeDtypeStruct((rows, wq.shape[1]), jnp.bfloat16),
            jax.ShapeDtypeStruct((rows, 2 * HEAD), jnp.bfloat16),
        ],
    )(piece, wq, wk, wv, cosine, sine)


def score(q, k):
    return lax.dot_general(q, k, (((1,), (1,)), ((), ())), preferred_element_type=jnp.float32)


def attend_kernel(
    n_blocks, chunk, heads, mask_ref, q_ref, kv_ref, out_ref, near, stream, sem, stream_sem
):
    blk = lax.axis_index("blk")
    rows = q_ref.shape[0] // BLOCK
    lanes = lax.broadcasted_iota(jnp.int32, (1, n_blocks), 1)
    copies = []
    for r in range(rows):
        i = blk * rows + r
        live = mask_ref[r : r + 1, :] != 0
        fixed = (jnp.abs(lanes - i) <= 1) | (lanes < 1)
        left = jnp.where(live & jnp.logical_not(fixed), lanes, n_blocks)
        ids = [0, jnp.maximum(i - 1, 0), i, jnp.minimum(i + 1, n_blocks - 1)]
        last = jnp.int32(-1)
        for _ in range(3):
            last = jnp.min(jnp.where(left > last, left, n_blocks))
            ids.append(jnp.minimum(last, n_blocks - 1))
        for s, j in enumerate(ids):
            copies.append(
                pltpu.make_async_copy(
                    kv_ref.at[pl.ds(pl.multiple_of(j * BLOCK, BLOCK), BLOCK)],
                    near.at[r, pl.ds(s * BLOCK, BLOCK)],
                    sem.at[r, s],
                )
            )
            copies[-1].start()
    slots = len(copies) // rows

    def queries(r):
        return jnp.concatenate(
            [
                q_ref[r * BLOCK : (r + 1) * BLOCK, h * HEAD : (h + 1) * HEAD]
                for h in range(heads)
            ],
            axis=0,
        )

    def put(r, mixed):
        for h in range(heads):
            out_ref[r * BLOCK : (r + 1) * BLOCK, h * HEAD : (h + 1) * HEAD] = mixed[
                h * BLOCK : (h + 1) * BLOCK
            ].astype(jnp.bfloat16)

    for r in range(rows):
        i = blk * rows + r
        for s in range(slots):
            copies[r * slots + s].wait()
        s = score(queries(r), near[r, :, :HEAD])
        parts = [
            jnp.where(i == 1, NEG, s[:, :BLOCK]),
            s[:, BLOCK : 3 * BLOCK],
            jnp.where(i == n_blocks - 1, NEG, s[:, 3 * BLOCK : 4 * BLOCK]),
            s[:, 4 * BLOCK :],
        ]
        s = jnp.concatenate(parts, axis=1)
        top = jnp.max(s, axis=1, keepdims=True)
        p = jnp.exp2(s * SCALE2 - top * SCALE2)
        total = jnp.sum(p, axis=1, keepdims=True)
        mixed = jnp.dot(
            p.astype(jnp.bfloat16), near[r, :, HEAD:], preferred_element_type=jnp.float32
        )
        put(r, mixed / total)

    @pl.when(blk == 0)
    def _():
        keys = chunk * BLOCK
        steps = n_blocks // chunk

        def fetch(step, slot):
            return pltpu.make_async_copy(
                kv_ref.at[pl.ds(pl.multiple_of(step * keys, keys), keys)],
                stream.at[slot],
                stream_sem.at[slot],
            )

        fetch(0, 0).start()
        q = queries(0)
        n = q.shape[0]

        def body(step, state):
            top, total, accum = state
            slot = lax.rem(step, 2)
            fetch(step, slot).wait()

            @pl.when(step + 1 < steps)
            def _():
                fetch(step + 1, 1 - slot).start()

            s = score(q, stream[slot, :, :HEAD])
            new = jnp.maximum(top, jnp.max(s, axis=1, keepdims=True))
            p = jnp.exp2(s * SCALE2 - new * SCALE2)
            factor = jnp.exp2((top - new) * SCALE2)
            total = total * factor + jnp.sum(p, axis=1, keepdims=True)
            accum = accum * factor + jnp.dot(
                p.astype(jnp.bfloat16),
                stream[slot, :, HEAD:],
                preferred_element_type=jnp.float32,
            )
            return new, total, accum

        top, total, accum = lax.fori_loop(
            0,
            steps,
            body,
            (
                jnp.full((n, 1), NEG, jnp.float32),
                jnp.zeros((n, 1), jnp.float32),
                jnp.zeros((n, HEAD), jnp.float32),
            ),
        )
        put(0, accum / total)


def attend(block_mask, q, kv):
    rows = q.shape[0] // BLOCK
    n_blocks = kv.shape[0] // BLOCK
    heads = q.shape[1] // HEAD
    chunk = 8
    vmem = pl.BlockSpec(memory_space=pltpu.VMEM)
    return pl.pallas_call(
        functools.partial(attend_kernel, n_blocks, chunk, heads),
        in_specs=[vmem, vmem, pl.BlockSpec(memory_space=pl.ANY)],
        out_specs=vmem,
        out_shape=jax.ShapeDtypeStruct(q.shape, jnp.bfloat16),
        scratch_shapes=[
            pltpu.VMEM((rows, 7 * BLOCK, 2 * HEAD), jnp.bfloat16),
            pltpu.VMEM((2, chunk * BLOCK, 2 * HEAD), jnp.bfloat16),
            pltpu.SemaphoreType.DMA((rows, 7)),
            pltpu.SemaphoreType.DMA((2,)),
        ],
    )(block_mask, q, kv)


def body(tokens, w_query, key_weight, value_weight, w_output, block_mask, positions):
    cosine, sine = rotary_tables(positions)
    piece = lax.all_gather(tokens, "grp", axis=0, tiled=True)
    q, kv = project(piece, w_query, key_weight, value_weight, cosine, sine)
    kv = lax.all_gather(kv, "blk", axis=0, tiled=True)
    mixed = attend(block_mask, q, kv)
    term = jnp.dot(mixed, w_output, preferred_element_type=jnp.float32)
    return lax.psum_scatter(
        term.astype(jnp.bfloat16), "grp", scatter_dimension=0, tiled=True
    )


def solution(mesh):
    return jax.shard_map(
        body,
        mesh=mesh,
        in_specs=(
            P(("blk", "grp"), None),
            P(None, "grp"),
            P(None, "grp"),
            P(None, "grp"),
            P("grp", None),
            P("blk", None),
            P("blk"),
        ),
        out_specs=P(("blk", "grp"), None),
        check_vma=False,
    )
```

time: 1000 us -> 297 us (0.30)
  local copies, waits for them, and re-layouts: 321 us -> 0 us
  other arithmetic: 182 us -> 2.71 us
  loops' own time: 99.9 us -> 0 us
  matrix products: 91.2 us -> 6.66 us
  waiting for transfers between devices: 284 us -> 237 us
  Pallas kernels: 0 us -> 38 us
    squeeze x288 -> x0, local copies, waits for them, and re-layouts: 108 us -> none  [the longest x256 76.6 us: fold_tiles(): lax.scan(over_query, 0, (query_tiles, fold_state[0], fold_state[1], fold_...]
    another operation x161 -> x0, loops' own time: 99.9 us -> none  [the longest x32 76.5 us: fold_tiles(): lax.scan(over_query, 0, (query_tiles, fold_state[0], fold_state[1], fold_...]
    while x129 -> x0, local copies, waits for them, and re-layouts: 93.7 us -> none
    dynamic_update_slice x384 -> x0, local copies, waits for them, and re-layouts: 93.6 us -> none  [fold_tiles(): lax.scan(over_query, 0, (query_tiles, fold_state[0], fold_state[1], fold_...]
    dot_general x93 -> x0, matrix products: 84.7 us -> none  [the longest x45 56.5 us: attend(): jnp.einsum('crg,gcd->crd', weights.astype(jnp.bfloat16), value_tile, pref...]
    reduce_or x128 -> x0, other arithmetic: 80.6 us -> none  [over_query(): jnp.any(live_blocks)]
    all_gather x2 -> x1, waiting for transfers between devices: 116 us -> 70.8 us  [body(): kv = lax.all_gather(kv, 'blk', axis=0, tiled=True)]
    reduce_sum x45 -> x0, other arithmetic: 40.1 us -> none  [attend(): total_new = total_old * factor + jnp.sum(weights, axis=-1)]
  transfers between devices with their start and end apart: 4 -> 3, of which waited for: 4 -> 3; matrix products, arithmetic and copies ran while one was open for 2% -> 1% of each run, Pallas kernels for 0% -> 0%
where the time goes in v1:
time: 297 us
  waiting for transfers between devices  237 us (80%)
  Pallas kernels  38 us (13%)
  between operations  13.1 us (4%)
  matrix products  6.66 us (2%)
    reduce_scatter x1, waiting for transfers between devices, body(): lax.psum_scatter(term.astype(jnp.bfloat16), 'grp', scatter_dimension=0, t...  86.6 us
    all_gather x1, waiting for transfers between devices, body(): piece = lax.all_gather(tokens, 'grp', axis=0, tiled=True)  78.4 us
    all_gather x1, waiting for transfers between devices, body(): kv = lax.all_gather(kv, 'blk', axis=0, tiled=True)  70.8 us
    pallas_call x1, Pallas kernels, attend(): pl.pallas_call(functools.partial(attend_kernel, n_blocks, chunk, heads),...  28.7 us
    pallas_call x1, Pallas kernels, project(): pl.pallas_call(project_kernel, grid=(rows // step,), in_specs=[pl.BlockSp...  9.28 us
    dot_general x1, matrix products, body(): term = jnp.dot(mixed, w_output, preferred_element_type=jnp.float32)  6.66 us
  transfers between devices with their start and end apart: 3, of which 3 were waited for; matrix products, arithmetic and copies ran while one was open for 1% of the time, Pallas kernels for 0%

profile of v1, /device:TPU:2, one launch (start us, length us, event | category | flops | bytes accessed | tf_op | source)
XLA Modules:
  0.0 297.2 jit_solution(10690033850966369122)
XLA Ops:
  6.5 0.0 all-gather.3.cloned.1.call-start
  6.5 0.7 all-gather.3.cloned.1.call-update
  7.3 0.0 all-gather.5.cloned.1.call-start
  7.3 0.7 convert_element_type.6
  8.0 1.0 fusion
  9.0 1.0 pad_maximum_fusion
  10.0 78.4 %all-gather.3.cloned.1.call-done.x_ref = bf16[512,4096]{1,0:T(8,128)(2,1)} async-done(((bf16[64,4096]{1,0:T(8,128)(2,1)}), bf16[512,4096]{1,0:T(8,128)(2,1)}) %all-gather.3.cloned.1.call-update) | async-done | bytes 4194320 | tf_op jit(solution)/shard_map/all_gather | solution.py:211
  88.4 9.3 %shard_map.73 = (bf16[512,512]{1,0:T(8,128)(2,1)}, bf16[512,256]{1,0:T(8,128)(2,1)}) custom-call(bf16[512,4096]{1,0:T(8,128)(2,1)} %all-gather.3.cloned.1.call-done.x_ref, bf16[4096,512]{1,0:T(8,128)(2,1)} %wq_ref.1, bf16[4096,128]{1,0:T(8,128)(2,1)} %wk_ref.1, bf16[4096,128]{1,0:T(8,128)(2,1)} %wv_ref.1, f32[512,128]{1,0:T(8,128)} %get-tuple-element.12.cos_ref, ...), custom_call_target="tpu_custom_call" | custom-call | tf_op jit(solution)/shard_map/pallas_call | solution.py:50
  97.7 0.0 all-gather.5.cloned.1.call-update
  97.7 0.0 reduce-scatter.2.cloned.1.call-start
  97.8 70.8 %all-gather.5.cloned.1.call-done.kv_ref = bf16[16384,256]{1,0:T(8,128)(2,1)} async-done(((bf16[512,256]{1,0:T(8,128)(2,1)}), bf16[16384,256]{1,0:T(8,128)(2,1)}) %all-gather.5.cloned.1.call-update) | async-done | bytes 8388624 | tf_op jit(solution)/shard_map/all_gather | solution.py:213
  168.6 28.7 %shard_map.74 = bf16[512,512]{1,0:T(8,128)(2,1)} custom-call(s32[4,128]{1,0:T(4,128)} %mask_ref.1, bf16[512,512]{1,0:T(8,128)(2,1)} %get-tuple-element.7.q_ref, bf16[16384,256]{1,0:T(8,128)(2,1)} %all-gather.5.cloned.1.call-done.kv_ref), custom_call_target="tpu_custom_call" | custom-call | tf_op jit(solution)/shard_map/pallas_call | solution.py:195
  197.3 6.7 %convolution_convert_fusion = bf16[512,4096]{1,0:T(8,128)(2,1)} fusion(bf16[512,512]{1,0:T(8,128)(2,1)} %shard_map.74, bf16[512,4096]{1,0:T(8,128)(2,1)} %param.11), kind=kOutput, calls=%fused_computation | convolution fusion | flops 2149580800 | bytes 8912896 | tf_op jit(solution)/shard_map/dot_general | solution.py:215
  204.0 0.0 reduce-scatter.2.cloned.1.call-update
  204.0 86.6 %reduce-scatter.2.cloned.1.call-done = bf16[64,4096]{1,0:T(8,128)(2,1)} async-done(((bf16[512,4096]{1,0:T(8,128)(2,1)}), bf16[64,4096]{1,0:T(8,128)(2,1)}) %reduce-scatter.2.cloned.1.call-update) | async-done | bytes 524304 | tf_op jit(solution)/shard_map/reduce_scatter | solution.py:216
  (1 shorter events, 0.0 us)
Async XLA Ops:
  6.5 81.9 %all-gather.3.cloned.1.call-start = ((), (), s32[]{:S(2)}) async-start(), calls=%async_computation.1 | async-start | bytes 4718592 | tf_op jit(solution)/shard_map/all_gather | solution.py:211
  7.3 161.4 %all-gather.5.cloned.1.call-start = ((), (), s32[]{:S(2)}) async-start(), calls=%async_computation.2 | async-start | bytes 8650752 | tf_op jit(solution)/shard_map/all_gather | solution.py:213
  97.7 192.9 %reduce-scatter.2.cloned.1.call-start = ((), (), s32[]{:S(2)}) async-start(), calls=%async_computation.3 | async-start | bytes 4718592 | tf_op jit(solution)/shard_map/reduce_scatter | solution.py:216
Sparse Core Ops, SparseCore 0:
  10.0 78.4 all-gather.2
  97.8 70.7 all-gather.4
  204.1 86.4 reduce-scatter.1

commit v2 on v1

--- a/solution.py
+++ b/solution.py
@@ -206,16 +206,162 @@
     )(block_mask, q, kv)
 
 
+MESH_ID = pl.DeviceIdType.MESH
+RING = 4
+HALVES = 2
+
+
+def places():
+    g = lax.axis_index("grp")
+    col, row = lax.rem(g, RING), g // RING
+
+    def at(dc, flip):
+        r = 1 - row if flip else row
+        return r * RING + lax.rem(col + dc + RING, RING)
+
+    return at
+
+
+def greet(peers):
+    barrier = pltpu.get_barrier_semaphore()
+    for peer in peers:
+        pl.semaphore_signal(barrier, inc=1, device_id=peer, device_id_type=MESH_ID)
+    pl.semaphore_wait(barrier, len(peers))
+
+
+def reduce_kernel(
+    shard, mixed_ref, w_ref, out_ref,
+    terms, far_in, near_in, pair_out, pair_in,
+    far_send, far_recv, near_send, near_recv, pair_send, pair_recv,
+):
+    at = places()
+    right, left, pair = at(1, False), at(-1, False), at(0, True)
+    side = ({"grp": right}, {"grp": left})
+    width = w_ref.shape[1] // HALVES
+    FAR, RIGHT, LEFT, OWN = 0, 1, 2, 3
+    greet([side[0], side[1], {"grp": pair}])
+
+    def product(slot, dc):
+        lhs = jnp.concatenate(
+            [
+                mixed_ref[pl.ds(pl.multiple_of(at(dc, flip) * shard, shard), shard), :]
+                for flip in (True, False)
+            ],
+            axis=0,
+        )
+        step = 512
+        for half in range(HALVES):
+            for c in range(width // step):
+                cols = slice(c * step, (c + 1) * step)
+                wide = slice(half * width + c * step, half * width + (c + 1) * step)
+                t = jnp.dot(lhs, w_ref[:, wide], preferred_element_type=jnp.float32)
+                for row in range(2):
+                    terms[slot, row, half, :, cols] = t[
+                        row * shard : (row + 1) * shard
+                    ].astype(jnp.bfloat16)
+
+    def far(row, way):
+        return pltpu.make_async_remote_copy(
+            terms.at[FAR, row, way], far_in.at[way, row],
+            far_send.at[way, row], far_recv.at[way, row],
+            device_id=side[way], device_id_type=MESH_ID,
+        )
+
+    def near(row, way, half):
+        return pltpu.make_async_remote_copy(
+            terms.at[RIGHT + way, row, half], near_in.at[way, row, half],
+            near_send.at[way, row, half], near_recv.at[way, row, half],
+            device_id=side[way], device_id_type=MESH_ID,
+        )
+
+    def across(half):
+        return pltpu.make_async_remote_copy(
+            pair_out.at[half], pair_in.at[half], pair_send.at[half], pair_recv.at[half],
+            device_id={"grp": pair}, device_id_type=MESH_ID,
+        )
+
+    def carry(row, way):
+        far(row, way).wait_recv()
+        slot = RIGHT + way
+        terms[slot, row, way] = (
+            terms[slot, row, way].astype(jnp.float32) + far_in[way, row].astype(jnp.float32)
+        ).astype(jnp.bfloat16)
+        near(row, way, way).start()
+
+    def gathered(row, half):
+        near(row, 0, half).wait_recv()
+        near(row, 1, half).wait_recv()
+        return (
+            terms[OWN, row, half].astype(jnp.float32)
+            + near_in[0, row, half].astype(jnp.float32)
+            + near_in[1, row, half].astype(jnp.float32)
+        )
+
+    product(FAR, 2)
+    far(0, 0).start()
+    far(0, 1).start()
+    product(RIGHT, 1)
+    near(0, 0, 1).start()
+    product(LEFT, -1)
+    near(0, 1, 0).start()
+    carry(0, 0)
+    carry(0, 1)
+    far(1, 0).start()
+    far(1, 1).start()
+    near(1, 0, 1).start()
+    near(1, 1, 0).start()
+    product(OWN, 0)
+    for half in range(HALVES):
+        pair_out[half] = gathered(0, half).astype(jnp.bfloat16)
+        across(half).start()
+    carry(1, 0)
+    carry(1, 1)
+    for half in range(HALVES):
+        total = gathered(1, half)
+        across(half).wait_recv()
+        total = total + pair_in[half].astype(jnp.float32)
+        out_ref[:, half * width : (half + 1) * width] = total.astype(jnp.bfloat16)
+    for row in range(2):
+        for way in range(2):
+            far(row, way).wait_send()
+            for half in range(HALVES):
+                near(row, way, half).wait_send()
+    for half in range(HALVES):
+        across(half).wait_send()
+
+
+def reduce_out(mixed, w_output, groups):
+    rows, width = mixed.shape[0], w_output.shape[1]
+    shard, half = rows // groups, width // HALVES
+    vmem = pl.BlockSpec(memory_space=pltpu.VMEM)
+    dma = pltpu.SemaphoreType.DMA
+    piece = (shard, half)
+    return pl.pallas_call(
+        functools.partial(reduce_kernel, shard),
+        in_specs=[vmem, vmem],
+        out_specs=vmem,
+        out_shape=jax.ShapeDtypeStruct((shard, width), jnp.bfloat16),
+        scratch_shapes=[
+            pltpu.VMEM((4, 2, HALVES, *piece), jnp.bfloat16),
+            pltpu.VMEM((2, 2, *piece), jnp.bfloat16),
+            pltpu.VMEM((2, 2, HALVES, *piece), jnp.bfloat16),
+            pltpu.VMEM((HALVES, *piece), jnp.bfloat16),
+            pltpu.VMEM((HALVES, *piece), jnp.bfloat16),
+            dma((2, 2)), dma((2, 2)),
+            dma((2, 2, HALVES)), dma((2, 2, HALVES)),
+            dma((HALVES,)), dma((HALVES,)),
+        ],
+        compiler_params=pltpu.CompilerParams(collective_id=1, has_side_effects=True),
+    )(mixed, w_output)
+
+
 def body(tokens, w_query, key_weight, value_weight, w_output, block_mask, positions):
     cosine, sine = rotary_tables(positions)
     piece = lax.all_gather(tokens, "grp", axis=0, tiled=True)
     q, kv = project(piece, w_query, key_weight, value_weight, cosine, sine)
     kv = lax.all_gather(kv, "blk", axis=0, tiled=True)
     mixed = attend(block_mask, q, kv)
-    term = jnp.dot(mixed, w_output, preferred_element_type=jnp.float32)
-    return lax.psum_scatter(
-        term.astype(jnp.bfloat16), "grp", scatter_dimension=0, tiled=True
-    )
+    return reduce_out(mixed, w_output, lax.axis_size("grp"))
 
 
 def solution(mesh):

time: 297 us -> 235 us (0.79)
  waiting for transfers between devices: 237 us -> 150 us
  Pallas kernels: 38 us -> 66.3 us
  matrix products: 6.66 us -> 0 us
    reduce_scatter x1 -> x0, waiting for transfers between devices: 86.6 us -> none  [body(): lax.psum_scatter(term.astype(jnp.bfloat16), 'grp', scatter_dimension=0, t...]
    pallas_call x0 -> x1, Pallas kernels: none -> 28.2 us  [reduce_out(): pl.pallas_call(functools.partial(reduce_kernel, shard), in_specs=[vmem, v...]
    dot_general x1 -> x0, matrix products: 6.66 us -> none  [body(): term = jnp.dot(mixed, w_output, preferred_element_type=jnp.float32)]
  transfers between devices with their start and end apart: 3 -> 2, of which waited for: 3 -> 2; matrix products, arithmetic and copies ran while one was open for 1% -> 1% of each run, Pallas kernels for 0% -> 0%
where the time goes in v2:
time: 235 us; the launch traced here: 234 us
  waiting for transfers between devices  150 us (64%)
  Pallas kernels  66.3 us (28%)
  between operations  13.4 us (6%)
  other arithmetic  2.71 us (1%)
    all_gather x1, waiting for transfers between devices, body(): piece = lax.all_gather(tokens, 'grp', axis=0, tiled=True)  78.4 us
    all_gather x1, waiting for transfers between devices, body(): kv = lax.all_gather(kv, 'blk', axis=0, tiled=True)  70.9 us
    pallas_call x1, Pallas kernels, attend(): pl.pallas_call(functools.partial(attend_kernel, n_blocks, chunk, heads),...  28.8 us
    pallas_call x1, Pallas kernels, reduce_out(): pl.pallas_call(functools.partial(reduce_kernel, shard), in_specs=[vmem, v...  28.2 us
    pallas_call x1, Pallas kernels, project(): pl.pallas_call(project_kernel, grid=(rows // step,), in_specs=[pl.BlockSp...  9.28 us
  transfers between devices with their start and end apart: 2, of which 2 were waited for; matrix products, arithmetic and copies ran while one was open for 1% of the time, Pallas kernels for 0%

profile of v2, /device:TPU:2, one launch (start us, length us, event | category | flops | bytes accessed | tf_op | source)
XLA Modules:
  0.0 234.4 jit_solution(8331970845956301320)
XLA Ops:
  6.5 0.0 all-gather.3.cloned.1.call-start
  6.5 0.7 all-gather.3.cloned.1.call-update
  7.3 0.0 all-gather.5.cloned.1.call-start
  7.3 0.7 convert_element_type.3
  8.0 1.0 fusion
  9.0 1.0 pad_maximum_fusion
  10.0 78.4 %all-gather.3.cloned.1.call-done.x_ref = bf16[512,4096]{1,0:T(8,128)(2,1)} async-done(((bf16[64,4096]{1,0:T(8,128)(2,1)}), bf16[512,4096]{1,0:T(8,128)(2,1)}) %all-gather.3.cloned.1.call-update) | async-done | bytes 4194320 | tf_op jit(solution)/shard_map/all_gather | solution.py:360
  88.4 9.3 %shard_map.73 = (bf16[512,512]{1,0:T(8,128)(2,1)}, bf16[512,256]{1,0:T(8,128)(2,1)}) custom-call(bf16[512,4096]{1,0:T(8,128)(2,1)} %all-gather.3.cloned.1.call-done.x_ref, bf16[4096,512]{1,0:T(8,128)(2,1)} %wq_ref.1, bf16[4096,128]{1,0:T(8,128)(2,1)} %wk_ref.1, bf16[4096,128]{1,0:T(8,128)(2,1)} %wv_ref.1, f32[512,128]{1,0:T(8,128)} %get-tuple-element.12.cos_ref, ...), custom_call_target="tpu_custom_call" | custom-call | tf_op jit(solution)/shard_map/pallas_call | solution.py:50
  97.7 0.0 all-gather.5.cloned.1.call-update
  97.7 70.9 %all-gather.5.cloned.1.call-done.kv_ref = bf16[16384,256]{1,0:T(8,128)(2,1)} async-done(((bf16[512,256]{1,0:T(8,128)(2,1)}), bf16[16384,256]{1,0:T(8,128)(2,1)}) %all-gather.5.cloned.1.call-update) | async-done | bytes 8388624 | tf_op jit(solution)/shard_map/all_gather | solution.py:362
  168.6 28.8 %shard_map.74.mixed_ref = bf16[512,512]{1,0:T(8,128)(2,1)} custom-call(s32[4,128]{1,0:T(4,128)} %mask_ref.1, bf16[512,512]{1,0:T(8,128)(2,1)} %get-tuple-element.7.q_ref, bf16[16384,256]{1,0:T(8,128)(2,1)} %all-gather.5.cloned.1.call-done.kv_ref), custom_call_target="tpu_custom_call" | custom-call | tf_op jit(solution)/shard_map/pallas_call | solution.py:195
  197.5 28.2 %shard_map.75 = bf16[64,4096]{1,0:T(8,128)(2,1)} custom-call(bf16[512,512]{1,0:T(8,128)(2,1)} %shard_map.74.mixed_ref, bf16[512,4096]{1,0:T(8,128)(2,1)} %w_ref.1), custom_call_target="tpu_custom_call" | custom-call | tf_op jit(solution)/shard_map/pallas_call | solution.py:339
  225.6 1.9 copy.9
  (1 shorter events, 0.0 us)
Async XLA Ops:
  6.5 81.9 %all-gather.3.cloned.1.call-start = ((), (), s32[]{:S(2)}) async-start(), calls=%async_computation | async-start | bytes 4718592 | tf_op jit(solution)/shard_map/all_gather | solution.py:360
  7.3 161.4 %all-gather.5.cloned.1.call-start = ((), (), s32[]{:S(2)}) async-start(), calls=%async_computation.1 | async-start | bytes 8650752 | tf_op jit(solution)/shard_map/all_gather | solution.py:362
Sparse Core Ops, SparseCore 0:
  10.0 78.4 all-gather.2
  97.8 70.7 all-gather.4

commit v3 on v2

--- a/solution.py
+++ b/solution.py
@@ -31,55 +31,18 @@
     return v * cosine + pltpu.roll(v, HEAD // 2, 1) * sine
 
 
-def project_kernel(x_ref, wq_ref, wk_ref, wv_ref, cos_ref, sin_ref, q_ref, kv_ref):
-    cosine, sine = cos_ref[...], sin_ref[...]
-    x = x_ref[...]
-    k = jnp.dot(x, wk_ref[...], preferred_element_type=jnp.float32)
-    kv_ref[:, :HEAD] = turn(k, cosine, sine).astype(jnp.bfloat16)
-    v = jnp.dot(x, wv_ref[...], preferred_element_type=jnp.float32)
-    kv_ref[:, HEAD:] = v.astype(jnp.bfloat16)
-    q = jnp.dot(x, wq_ref[...], preferred_element_type=jnp.float32)
-    for h in range(wq_ref.shape[1] // HEAD):
-        cols = slice(h * HEAD, (h + 1) * HEAD)
-        q_ref[:, cols] = turn(q[:, cols], cosine, sine).astype(jnp.bfloat16)
-
-
-def project(piece, wq, wk, wv, cosine, sine):
-    rows = piece.shape[0]
-    step = 128
-    return pl.pallas_call(
-        project_kernel,
-        grid=(rows // step,),
-        in_specs=[
-            pl.BlockSpec((step, piece.shape[1]), lambda i: (i, 0)),
-            pl.BlockSpec(wq.shape, lambda i: (0, 0)),
-            pl.BlockSpec(wk.shape, lambda i: (0, 0)),
-            pl.BlockSpec(wv.shape, lambda i: (0, 0)),
-            pl.BlockSpec((step, HEAD), lambda i: (i, 0)),
-            pl.BlockSpec((step, HEAD), lambda i: (i, 0)),
-        ],
-        out_specs=[
-            pl.BlockSpec((step, wq.shape[1]), lambda i: (i, 0)),
-            pl.BlockSpec((step, 2 * HEAD), lambda i: (i, 0)),
-        ],
-        out_shape=[
-            jax.ShapeDtypeStruct((rows, wq.shape[1]), jnp.bfloat16),
-            jax.ShapeDtypeStruct((rows, 2 * HEAD), jnp.bfloat16),
-        ],
-    )(piece, wq, wk, wv, cosine, sine)
-
-
 def score(q, k):
     return lax.dot_general(q, k, (((1,), (1,)), ((), ())), preferred_element_type=jnp.float32)
 
 
 def attend_kernel(
-    n_blocks, chunk, heads, mask_ref, q_ref, kv_ref, out_ref, near, stream, sem, stream_sem
+    n_blocks, heads, mask_ref, q_ref, kv_ref, out_ref, near, stream, sem, stream_sem
 ):
     blk = lax.axis_index("blk")
     rows = q_ref.shape[0] // BLOCK
+    shard = kv_ref.shape[4]
+    pieces = BLOCK // shard
     lanes = lax.broadcasted_iota(jnp.int32, (1, n_blocks), 1)
-    copies = []
     for r in range(rows):
         i = blk * rows + r
         live = mask_ref[r : r + 1, :] != 0
@@ -91,15 +54,18 @@
             last = jnp.min(jnp.where(left > last, left, n_blocks))
             ids.append(jnp.minimum(last, n_blocks - 1))
         for s, j in enumerate(ids):
-            copies.append(
+            owner = j // rows
+            for h in range(pieces):
                 pltpu.make_async_copy(
-                    kv_ref.at[pl.ds(pl.multiple_of(j * BLOCK, BLOCK), BLOCK)],
-                    near.at[r, pl.ds(s * BLOCK, BLOCK)],
-                    sem.at[r, s],
-                )
-            )
-            copies[-1].start()
-    slots = len(copies) // rows
+                    kv_ref.at[
+                        lax.rem(owner, 2),
+                        owner // 4,
+                        lax.rem(j, rows) * pieces + h,
+                        lax.rem(owner // 2, 2),
+                    ],
+                    near.at[r, pl.ds(s * BLOCK + h * shard, shard)],
+                    sem.at[r],
+                ).start()
 
     def queries(r):
         return jnp.concatenate(
@@ -118,8 +84,7 @@
 
     for r in range(rows):
         i = blk * rows + r
-        for s in range(slots):
-            copies[r * slots + s].wait()
+        pltpu.make_async_copy(near.at[r], near.at[r], sem.at[r]).wait()
         s = score(queries(r), near[r, :, :HEAD])
         parts = [
             jnp.where(i == 1, NEG, s[:, :BLOCK]),
@@ -138,12 +103,11 @@
 
     @pl.when(blk == 0)
     def _():
-        keys = chunk * BLOCK
-        steps = n_blocks // chunk
+        steps = kv_ref.shape[0] * kv_ref.shape[1]
 
         def fetch(step, slot):
             return pltpu.make_async_copy(
-                kv_ref.at[pl.ds(pl.multiple_of(step * keys, keys), keys)],
+                kv_ref.at[step // kv_ref.shape[1], lax.rem(step, kv_ref.shape[1])],
                 stream.at[slot],
                 stream_sem.at[slot],
             )
@@ -161,14 +125,15 @@
             def _():
                 fetch(step + 1, 1 - slot).start()
 
-            s = score(q, stream[slot, :, :HEAD])
+            both = stream[slot].reshape(-1, 2 * HEAD)
+            s = score(q, both[:, :HEAD])
             new = jnp.maximum(top, jnp.max(s, axis=1, keepdims=True))
             p = jnp.exp2(s * SCALE2 - new * SCALE2)
             factor = jnp.exp2((top - new) * SCALE2)
             total = total * factor + jnp.sum(p, axis=1, keepdims=True)
             accum = accum * factor + jnp.dot(
                 p.astype(jnp.bfloat16),
-                stream[slot, :, HEAD:],
+                both[:, HEAD:],
                 preferred_element_type=jnp.float32,
             )
             return new, total, accum
@@ -188,19 +153,18 @@
 
 def attend(block_mask, q, kv):
     rows = q.shape[0] // BLOCK
-    n_blocks = kv.shape[0] // BLOCK
+    n_blocks = block_mask.shape[1]
     heads = q.shape[1] // HEAD
-    chunk = 8
     vmem = pl.BlockSpec(memory_space=pltpu.VMEM)
     return pl.pallas_call(
-        functools.partial(attend_kernel, n_blocks, chunk, heads),
+        functools.partial(attend_kernel, n_blocks, heads),
         in_specs=[vmem, vmem, pl.BlockSpec(memory_space=pl.ANY)],
         out_specs=vmem,
         out_shape=jax.ShapeDtypeStruct(q.shape, jnp.bfloat16),
         scratch_shapes=[
             pltpu.VMEM((rows, 7 * BLOCK, 2 * HEAD), jnp.bfloat16),
-            pltpu.VMEM((2, chunk * BLOCK, 2 * HEAD), jnp.bfloat16),
-            pltpu.SemaphoreType.DMA((rows, 7)),
+            pltpu.VMEM((2, *kv.shape[2:]), jnp.bfloat16),
+            pltpu.SemaphoreType.DMA((rows,)),
             pltpu.SemaphoreType.DMA((2,)),
         ],
     )(block_mask, q, kv)
@@ -355,13 +319,284 @@
     )(mixed, w_output)
 
 
+Z_RING = 8
+
+
+def gather_kernel(
+    tokens_ref, wq_ref, wk_ref, wv_ref, cos_ref, sin_ref, q_ref, kv_ref,
+    tok, wq, wkv, mine,
+    load_sem, own_send, own_recv, far_send, far_recv,
+    mine_sem, y_send, y_recv, z_send, z_recv, core_send, core_recv,
+):
+    at = places()
+    side = ({"grp": at(1, False)}, {"grp": at(-1, False)})
+    pair = {"grp": at(0, True)}
+    blk = lax.axis_index("blk")
+    core, near_y, depth = lax.rem(blk, 2), lax.rem(blk // 2, 2), blk // 4
+    shard, half = tokens_ref.shape[0], tokens_ref.shape[0] // 2
+
+    def deep(step):
+        return lax.rem(depth + step + Z_RING, Z_RING)
+
+    z_side = tuple({"blk": (deep(d) * 2 + near_y) * 2 + core} for d in (1, -1))
+    y_side = {"blk": (depth * 2 + 1 - near_y) * 2 + core}
+    core_side = {"blk": (depth * 2 + near_y) * 2 + 1 - core}
+
+    loads = [
+        pltpu.make_async_copy(tokens_ref, tok.at[0, 0], load_sem.at[0]),
+        pltpu.make_async_copy(wk_ref, wkv.at[:, pl.ds(0, HEAD)], load_sem.at[1]),
+        pltpu.make_async_copy(wv_ref, wkv.at[:, pl.ds(HEAD, HEAD)], load_sem.at[2]),
+        pltpu.make_async_copy(wq_ref, wq, load_sem.at[3]),
+    ]
+    for load in loads:
+        load.start()
+    greet([*side, pair, *z_side, y_side, core_side])
+
+    def rows(row, place, h):
+        return tok.at[row, place, pl.ds(h * half, half)]
+
+    def hand(row, way, h):
+        return pltpu.make_async_remote_copy(
+            rows(row, 0, h), rows(row, 1 + way, h),
+            own_send.at[row, way, h], own_recv.at[row, way, h],
+            device_id=side[way], device_id_type=MESH_ID,
+        )
+
+    def cross(h):
+        return pltpu.make_async_remote_copy(
+            rows(0, 0, h), rows(1, 0, h), own_send.at[0, 2, h], own_recv.at[0, 2, h],
+            device_id=pair, device_id_type=MESH_ID,
+        )
+
+    def further(row, way):
+        return pltpu.make_async_remote_copy(
+            rows(row, 1 + way, way), rows(row, 3, way),
+            far_send.at[row, way], far_recv.at[row, way],
+            device_id=side[way], device_id_type=MESH_ID,
+        )
+
+    def hand_on(row):
+        for h in range(2):
+            hand(row, 0, h).start()
+            hand(row, 1, 1 - h).start()
+
+    def pass_on(row):
+        for way in range(2):
+            hand(row, way, way).wait_recv()
+            further(row, way).start()
+
+    order = ((0, 0, 0), (0, 1, -1), (0, 2, 1), (0, 3, 2), (1, 0, 0), (1, 1, -1), (1, 2, 1), (1, 3, 2))
+
+    def spot(u):
+        row, _, dc = order[u]
+        return at(dc, row == 1)
+
+    def tables(u):
+        here = pl.ds(pl.multiple_of(spot(u) * shard, shard), shard)
+        return cos_ref[here, :], sin_ref[here, :]
+
+    def keep(u):
+        return pltpu.make_async_copy(
+            mine.at[u], kv_ref.at[core, depth, spot(u), near_y], mine_sem.at[u]
+        )
+
+    def y_copy(u):
+        return pltpu.make_async_remote_copy(
+            mine.at[u], kv_ref.at[core, depth, spot(u), near_y],
+            y_send.at[u], y_recv.at[u],
+            device_id=y_side, device_id_type=MESH_ID,
+        )
+
+    def z_copy(u, way, hop):
+        origin = deep(-hop if way == 0 else hop)
+        ref = kv_ref.at[core, origin, spot(u)]
+        if hop == 3:
+            ref = kv_ref.at[core, origin, spot(u), way]
+        return pltpu.make_async_remote_copy(
+            ref, ref, z_send.at[way, hop, u], z_recv.at[way, hop, u],
+            device_id=z_side[way], device_id_type=MESH_ID,
+        )
+
+    def z_arrival(u, way, hop):
+        origin = deep(-hop - 1 if way == 0 else hop + 1)
+        ref = kv_ref.at[core, origin, spot(u)]
+        if hop == 3:
+            ref = kv_ref.at[core, origin, spot(u), way]
+        return pltpu.make_async_remote_copy(
+            ref, ref, z_send.at[way, hop, u], z_recv.at[way, hop, u],
+            device_id=z_side[way], device_id_type=MESH_ID,
+        )
+
+    def core_copy(u, origin):
+        ref = kv_ref.at[core, origin, spot(u)]
+        return pltpu.make_async_remote_copy(
+            ref, ref, core_send, core_recv, device_id=core_side, device_id_type=MESH_ID
+        )
+
+    def keys(u):
+        row, place, _ = order[u]
+        y = jnp.dot(tok[row, place], wkv[...], preferred_element_type=jnp.float32)
+        cosine, sine = tables(u)
+        mine[u, :, :HEAD] = turn(y[:, :HEAD], cosine, sine).astype(jnp.bfloat16)
+        mine[u, :, HEAD:] = y[:, HEAD:].astype(jnp.bfloat16)
+        keep(u).start()
+        y_copy(u).start()
+
+    def ring(u, stage):
+        if stage == 0:
+            keep(u).wait()
+            y_copy(u).wait_recv()
+            z_copy(u, 0, 0).start()
+            z_copy(u, 1, 0).start()
+            core_copy(u, depth).start()
+            return
+        for way in range(2):
+            z_arrival(u, way, stage - 1).wait_recv()
+            if stage < 4:
+                z_copy(u, way, stage).start()
+                core_copy(u, deep(-stage if way == 0 else stage)).start()
+        if stage == 4:
+            core_copy(u, deep(4)).start()
+
+    def queries(row, part):
+        wide = 2 * HEAD
+        x = tok[row].reshape(4 * shard, tok.shape[-1])
+        cols = slice(part * wide, (part + 1) * wide)
+        y = jnp.dot(x, wq[:, cols], preferred_element_type=jnp.float32)
+        for n in range(4):
+            u = next(i for i, o in enumerate(order) if o[:2] == (row, n))
+            cosine, sine = tables(u)
+            here = pl.ds(pl.multiple_of(spot(u) * shard, shard), shard)
+            for h in range(2):
+                v = y[n * shard : (n + 1) * shard, h * HEAD : (h + 1) * HEAD]
+                q_ref[here, part * wide + h * HEAD : part * wide + (h + 1) * HEAD] = turn(
+                    v, cosine, sine
+                ).astype(jnp.bfloat16)
+
+    loads[0].wait()
+    hand_on(0)
+    for h in range(2):
+        cross(h).start()
+    loads[1].wait()
+    loads[2].wait()
+    keys(0)
+    ring(0, 0)
+    pass_on(0)
+    ring(0, 1)
+    ring(0, 2)
+    hand(0, 0, 1).wait_recv()
+    keys(1)
+    hand(0, 1, 0).wait_recv()
+    keys(2)
+    ring(0, 3)
+    ring(1, 0)
+    ring(2, 0)
+    for h in range(2):
+        cross(h).wait_recv()
+    hand_on(1)
+    ring(0, 4)
+    ring(1, 1)
+    ring(2, 1)
+    further(0, 0).wait_recv()
+    further(0, 1).wait_recv()
+    keys(3)
+    keys(4)
+    ring(1, 2)
+    ring(2, 2)
+    ring(3, 0)
+    ring(4, 0)
+    loads[3].wait()
+    queries(0, 0)
+    ring(1, 3)
+    ring(2, 3)
+    ring(3, 1)
+    ring(4, 1)
+    queries(0, 1)
+    pass_on(1)
+    ring(1, 4)
+    ring(2, 4)
+    ring(3, 2)
+    ring(4, 2)
+    hand(1, 0, 1).wait_recv()
+    keys(5)
+    hand(1, 1, 0).wait_recv()
+    keys(6)
+    ring(3, 3)
+    ring(4, 3)
+    ring(5, 0)
+    ring(6, 0)
+    further(1, 0).wait_recv()
+    further(1, 1).wait_recv()
+    keys(7)
+    ring(3, 4)
+    ring(4, 4)
+    ring(5, 1)
+    ring(6, 1)
+    ring(7, 0)
+    queries(1, 0)
+    ring(5, 2)
+    ring(6, 2)
+    ring(7, 1)
+    queries(1, 1)
+    for stage in (3, 4):
+        ring(5, stage)
+        ring(6, stage)
+        ring(7, stage - 1)
+    ring(7, 4)
+
+    for h in range(2):
+        cross(h).wait_send()
+        for row in range(2):
+            for way in range(2):
+                hand(row, way, h).wait_send()
+    for row in range(2):
+        for way in range(2):
+            further(row, way).wait_send()
+    for u in range(len(order)):
+        y_copy(u).wait_send()
+        for way in range(2):
+            for hop in range(4):
+                z_copy(u, way, hop).wait_send()
+    done = kv_ref.at[core]
+    pltpu.make_async_copy(done, done, core_send).wait()
+    done = kv_ref.at[1 - core]
+    pltpu.make_async_copy(done, done, core_recv).wait()
+
+
+def gather(tokens, wq, wk, wv, cosine, sine, groups):
+    shard, width = tokens.shape
+    units = groups
+    hbm, vmem = pl.BlockSpec(memory_space=pl.ANY), pl.BlockSpec(memory_space=pltpu.VMEM)
+    dma = pltpu.SemaphoreType.DMA
+    return pl.pallas_call(
+        gather_kernel,
+        in_specs=[hbm, hbm, hbm, hbm, vmem, vmem],
+        out_specs=[vmem, hbm],
+        out_shape=[
+            jax.ShapeDtypeStruct((shard * groups, wq.shape[1]), jnp.bfloat16),
+            jax.ShapeDtypeStruct((2, Z_RING, groups, 2, shard, 2 * HEAD), jnp.bfloat16),
+        ],
+        scratch_shapes=[
+            pltpu.VMEM((2, RING, shard, width), jnp.bfloat16),
+            pltpu.VMEM(wq.shape, jnp.bfloat16),
+            pltpu.VMEM((width, 2 * HEAD), jnp.bfloat16),
+            pltpu.VMEM((units, shard, 2 * HEAD), jnp.bfloat16),
+            dma((4,)),
+            dma((2, 3, 2)), dma((2, 3, 2)), dma((2, 2)), dma((2, 2)),
+            dma((units,)), dma((units,)), dma((units,)),
+            dma((2, 4, units)), dma((2, 4, units)),
+            dma, dma,
+        ],
+        compiler_params=pltpu.CompilerParams(collective_id=0, has_side_effects=True),
+    )(tokens, wq, wk, wv, cosine, sine)
+
+
 def body(tokens, w_query, key_weight, value_weight, w_output, block_mask, positions):
     cosine, sine = rotary_tables(positions)
-    piece = lax.all_gather(tokens, "grp", axis=0, tiled=True)
-    q, kv = project(piece, w_query, key_weight, value_weight, cosine, sine)
-    kv = lax.all_gather(kv, "blk", axis=0, tiled=True)
+    groups = lax.axis_size("grp")
+    q, kv = gather(tokens, w_query, key_weight, value_weight, cosine, sine, groups)
     mixed = attend(block_mask, q, kv)
-    return reduce_out(mixed, w_output, lax.axis_size("grp"))
+    return reduce_out(mixed, w_output, groups)
 
 
 def solution(mesh):

time: 235 us -> 146 us (0.62)
  waiting for transfers between devices: 150 us -> 0 us
  Pallas kernels: 66.3 us -> 142 us
  between operations: 13.4 us -> 0.03 us
    all_gather x2 -> x0, waiting for transfers between devices: 149 us -> none  [the longest x1 78.4 us: body(): piece = lax.all_gather(tokens, 'grp', axis=0, tiled=True)]
    pallas_call x2, Pallas kernels: 38.1 us -> 115 us  [the longest x1 86 us: gather(): pl.pallas_call(gather_kernel, in_specs=[hbm, hbm, hbm, hbm, vmem, vmem],...]
  transfers between devices with their start and end apart: 2 -> 0, of which waited for: 2 -> 0; matrix products, arithmetic and copies ran while one was open for 1% -> 0% of each run, Pallas kernels for 0% -> 0%
where the time goes in v3:
time: 146 us
  Pallas kernels  142 us (97%)
  other arithmetic  2.7 us (2%)
  local copies, waits for them, and re-layouts  1.87 us (1%)
    pallas_call x1, Pallas kernels, gather(): pl.pallas_call(gather_kernel, in_specs=[hbm, hbm, hbm, hbm, vmem, vmem],...  86 us
    pallas_call x1, Pallas kernels, attend(): pl.pallas_call(functools.partial(attend_kernel, n_blocks, heads), in_spec...  28.5 us
    pallas_call x1, Pallas kernels, reduce_out(): pl.pallas_call(functools.partial(reduce_kernel, shard), in_specs=[vmem, v...  27.1 us

profile of v3, /device:TPU:2, one launch (start us, length us, event | category | flops | bytes accessed | tf_op | source)
XLA Modules:
  0.0 146.2 jit_solution(5851135339920264034)
XLA Ops:
  0.0 0.7 convert_element_type.3
  0.7 1.0 fusion
  1.7 1.0 pad_maximum_fusion
  2.7 86.0 %shard_map.73 = (bf16[512,512]{1,0:T(8,128)(2,1)}, bf16[2,8,8,2,64,256]{5,4,3,2,1,0:T(8,128)(2,1)}) custom-call(bf16[64,4096]{1,0:T(8,128)(2,1)} %tokens_ref.1, bf16[4096,512]{1,0:T(8,128)(2,1)} %wq_ref.1, bf16[4096,128]{1,0:T(8,128)(2,1)} %wk_ref.1, bf16[4096,128]{1,0:T(8,128)(2,1)} %wv_ref.1, f32[512,128]{1,0:T(8,128)} %get-tuple-element.12.cos_ref, ...), custom_call_target="tpu_custom_call" | custom-call | tf_op jit(solution)/shard_map/pallas_call | solution.py:571
  88.7 28.5 %shard_map.74.mixed_ref = bf16[512,512]{1,0:T(8,128)(2,1)} custom-call(s32[4,128]{1,0:T(4,128)} %mask_ref.1, bf16[512,512]{1,0:T(8,128)(2,1)} %get-tuple-element.7.q_ref, bf16[2,8,8,2,64,256]{5,4,3,2,1,0:T(8,128)(2,1)} %get-tuple-element.8.kv_ref), custom_call_target="tpu_custom_call" | custom-call | tf_op jit(solution)/shard_map/pallas_call | solution.py:159
  117.2 27.1 %shard_map.75 = bf16[64,4096]{1,0:T(8,128)(2,1)} custom-call(bf16[512,512]{1,0:T(8,128)(2,1)} %shard_map.74.mixed_ref, bf16[512,4096]{1,0:T(8,128)(2,1)} %w_ref.1), custom_call_target="tpu_custom_call" | custom-call | tf_op jit(solution)/shard_map/pallas_call | solution.py:303
  144.3 1.9 %copy.9 = bf16[64,4096]{1,0:T(8,128)(2,1)} copy(bf16[64,4096]{1,0:T(8,128)(2,1)} %shard_map.75) | data formatting | bytes 1048576
  (1 shorter events, 0.0 us)

commit v4 on v3

--- a/solution.py
+++ b/solution.py
@@ -320,13 +320,38 @@
 
 
 Z_RING = 8
+RELAY = False
+SPLIT = (0, 3, 4, 5, 7)
+ORDER = (
+    (2, 0, 0, 0), (4, 0, 0, 0), (5, 0, 0, 0), (4, 0, 1, 0), (4, 0, 1, 1), (0, 0, 0, 0),
+    (0, 0, 1, 0), (1, 0, 0, 0), (4, 0, 2, 0), (4, 0, 2, 1), (5, 0, 1, 0), (5, 0, 1, 1),
+    (4, 0, 3, 0), (2, 1, 0, 0), (1, 1, 0, 0), (2, 2, 0, 0), (2, 4, 0, 0), (4, 4, 0, 0),
+    (2, 3, 0, 0), (4, 3, 0, 0), (4, 2, 0, 0), (4, 1, 0, 0), (4, 0, 3, 1), (4, 0, 4, 0),
+    (5, 0, 2, 0), (5, 0, 2, 1), (5, 0, 3, 0), (4, 4, 1, 0), (4, 4, 1, 1), (5, 4, 0, 0),
+    (3, 0, 0, 0), (0, 1, 0, 0), (4, 3, 1, 0), (4, 3, 1, 1), (5, 0, 3, 1), (5, 3, 0, 0),
+    (3, 0, 1, 0), (4, 2, 1, 0), (4, 2, 1, 1), (4, 1, 1, 0), (4, 1, 1, 1), (4, 4, 2, 0),
+    (4, 4, 2, 1), (5, 0, 4, 0), (4, 3, 2, 0), (4, 3, 2, 1), (5, 3, 1, 0), (0, 1, 1, 0),
+    (2, 5, 0, 0), (2, 6, 0, 0), (4, 5, 0, 0), (4, 2, 2, 0), (4, 2, 2, 1), (4, 1, 2, 0),
+    (4, 4, 3, 0), (4, 4, 3, 1), (4, 1, 2, 1), (4, 3, 3, 0), (4, 3, 3, 1), (5, 3, 1, 1),
+    (5, 3, 2, 0), (5, 3, 2, 1), (5, 4, 1, 0), (5, 4, 1, 1), (5, 4, 2, 0), (5, 4, 2, 1),
+    (5, 5, 0, 0), (4, 6, 0, 0), (4, 5, 1, 0), (4, 5, 1, 1), (5, 4, 3, 0), (2, 7, 0, 0),
+    (4, 7, 0, 0), (4, 2, 3, 0), (4, 2, 3, 1), (4, 1, 3, 0), (4, 4, 4, 0), (4, 3, 4, 1),
+    (4, 1, 3, 1), (5, 3, 3, 0), (5, 3, 3, 1), (5, 4, 3, 1), (5, 5, 1, 0), (3, 1, 0, 0),
+    (4, 6, 1, 0), (4, 7, 1, 0), (4, 7, 1, 1), (4, 6, 1, 1), (4, 5, 2, 0), (4, 5, 2, 1),
+    (4, 2, 4, 0), (4, 2, 4, 1), (4, 1, 4, 0), (4, 1, 4, 1), (5, 3, 4, 1), (5, 4, 4, 0),
+    (5, 5, 1, 1), (5, 7, 0, 0), (3, 1, 1, 0), (4, 7, 2, 1), (4, 6, 2, 0), (5, 7, 1, 0),
+    (5, 7, 1, 1), (4, 7, 2, 0), (5, 5, 2, 0), (4, 6, 2, 1), (4, 5, 3, 0), (5, 5, 2, 1),
+    (4, 5, 3, 1), (4, 7, 3, 1), (5, 7, 2, 1), (4, 6, 3, 0), (5, 7, 2, 0), (4, 7, 3, 0),
+    (5, 5, 3, 0), (4, 6, 3, 1), (5, 5, 3, 1), (4, 5, 4, 1), (4, 7, 4, 1), (5, 7, 3, 1),
+    (4, 6, 4, 0), (5, 7, 3, 0), (4, 6, 4, 1), (5, 5, 4, 1), (5, 7, 4, 1),
+)
 
 
 def gather_kernel(
     tokens_ref, wq_ref, wk_ref, wv_ref, cos_ref, sin_ref, q_ref, kv_ref,
     tok, wq, wkv, mine,
     load_sem, own_send, own_recv, far_send, far_recv,
-    mine_sem, y_send, y_recv, z_send, z_recv, core_send, core_recv,
+    mine_sem, y_send, y_recv, z_send, z_recv, fwd_send, fwd_recv, core_send, core_recv,
 ):
     at = places()
     side = ({"grp": at(1, False)}, {"grp": at(-1, False)})
@@ -375,15 +400,24 @@
             device_id=side[way], device_id_type=MESH_ID,
         )
 
-    def hand_on(row):
-        for h in range(2):
-            hand(row, 0, h).start()
-            hand(row, 1, 1 - h).start()
-
-    def pass_on(row):
+    def relay(way):
+        return pltpu.make_async_remote_copy(
+            rows(0, 1 + way, way), rows(1, 1 + way, way),
+            own_send.at[1, way, way], own_recv.at[1, way, way],
+            device_id=pair, device_id_type=MESH_ID,
+        )
+
+    def pass_on(row, way):
+        hand(row, way, way).wait_recv()
+        further(row, way).start()
+        if RELAY and row == 0:
+            relay(way).start()
+
+    def cross_on(h):
+        cross(h).wait_recv()
         for way in range(2):
-            hand(row, way, way).wait_recv()
-            further(row, way).start()
+            if not (RELAY and way == h):
+                hand(1, way, h).start()
 
     order = ((0, 0, 0), (0, 1, -1), (0, 2, 1), (0, 3, 2), (1, 0, 0), (1, 1, -1), (1, 2, 1), (1, 3, 2))
 
@@ -407,31 +441,59 @@
             device_id=y_side, device_id_type=MESH_ID,
         )
 
-    def z_copy(u, way, hop):
+    def z_copy(u, way, hop, own=True):
         origin = deep(-hop if way == 0 else hop)
         ref = kv_ref.at[core, origin, spot(u)]
-        if hop == 3:
+        if u in SPLIT:
+            ref = kv_ref.at[core, origin, spot(u), near_y]
+        elif hop == 3:
             ref = kv_ref.at[core, origin, spot(u), way]
-        return pltpu.make_async_remote_copy(
-            ref, ref, z_send.at[way, hop, u], z_recv.at[way, hop, u],
+        source = mine.at[u] if u in SPLIT and hop == 0 and own else ref
+        return pltpu.make_async_remote_copy(
+            source, ref, z_send.at[way, hop, u], z_recv.at[way, hop, u],
             device_id=z_side[way], device_id_type=MESH_ID,
         )
 
     def z_arrival(u, way, hop):
         origin = deep(-hop - 1 if way == 0 else hop + 1)
         ref = kv_ref.at[core, origin, spot(u)]
-        if hop == 3:
+        if u in SPLIT:
+            ref = kv_ref.at[core, origin, spot(u), near_y]
+        elif hop == 3:
             ref = kv_ref.at[core, origin, spot(u), way]
         return pltpu.make_async_remote_copy(
             ref, ref, z_send.at[way, hop, u], z_recv.at[way, hop, u],
             device_id=z_side[way], device_id_type=MESH_ID,
         )
 
-    def core_copy(u, origin):
+    def core_copy(u, origin, y=None, source=None):
         ref = kv_ref.at[core, origin, spot(u)]
-        return pltpu.make_async_remote_copy(
-            ref, ref, core_send, core_recv, device_id=core_side, device_id_type=MESH_ID
-        )
+        if y is not None:
+            ref = kv_ref.at[core, origin, spot(u), y]
+        return pltpu.make_async_remote_copy(
+            ref if source is None else source, ref, core_send, core_recv,
+            device_id=core_side, device_id_type=MESH_ID,
+        )
+
+    def origin_of(stage, way):
+        return deep(-stage if way == 0 else stage)
+
+    def y_forward(u, stage, way):
+        ref = kv_ref.at[core, origin_of(stage, way), spot(u), near_y]
+        return pltpu.make_async_remote_copy(
+            ref, ref, fwd_send.at[u, way, stage - 1], fwd_recv.at[u, way, stage - 1],
+            device_id=y_side, device_id_type=MESH_ID,
+        )
+
+    def y_landed(u, stage, way):
+        ref = kv_ref.at[core, origin_of(stage, way), spot(u), 1 - near_y]
+        return pltpu.make_async_remote_copy(
+            ref, ref, fwd_send.at[u, way, stage - 1], fwd_recv.at[u, way, stage - 1],
+            device_id=y_side, device_id_type=MESH_ID,
+        )
+
+    def hops(u, stage, way):
+        return stage < 3 or (stage == 3 and (u not in SPLIT or way == u % 2))
 
     def keys(u):
         row, place, _ = order[u]
@@ -442,21 +504,37 @@
         keep(u).start()
         y_copy(u).start()
 
-    def ring(u, stage):
+    def ring(u, stage, way):
         if stage == 0:
-            keep(u).wait()
-            y_copy(u).wait_recv()
+            if u not in SPLIT:
+                keep(u).wait()
+                y_copy(u).wait_recv()
             z_copy(u, 0, 0).start()
             z_copy(u, 1, 0).start()
-            core_copy(u, depth).start()
+            if u in SPLIT:
+                core_copy(u, depth, near_y, mine.at[u]).start()
+            else:
+                core_copy(u, depth).start()
             return
-        for way in range(2):
-            z_arrival(u, way, stage - 1).wait_recv()
-            if stage < 4:
-                z_copy(u, way, stage).start()
-                core_copy(u, deep(-stage if way == 0 else stage)).start()
-        if stage == 4:
-            core_copy(u, deep(4)).start()
+        z_arrival(u, way, stage - 1).wait_recv()
+        if hops(u, stage, way):
+            z_copy(u, way, stage, False).start()
+        origin = origin_of(stage, way)
+        if u in SPLIT:
+            y_forward(u, stage, way).start()
+            core_copy(u, origin, near_y).start()
+        elif stage < 4:
+            core_copy(u, origin).start()
+        else:
+            core_copy(u, origin, way).start()
+
+    def landed(u, stage, way):
+        if stage == 0:
+            y_copy(u).wait_recv()
+            core_copy(u, depth, 1 - near_y).start()
+        else:
+            y_landed(u, stage, way).wait_recv()
+            core_copy(u, origin_of(stage, way), 1 - near_y).start()
 
     def queries(row, part):
         wide = 2 * HEAD
@@ -473,76 +551,42 @@
                     v, cosine, sine
                 ).astype(jnp.bfloat16)
 
+    def project_keys(u):
+        row, place, _ = order[u]
+        if u == 0:
+            loads[1].wait()
+            loads[2].wait()
+        elif place == 3:
+            further(row, 0).wait_recv()
+            further(row, 1).wait_recv()
+        elif place:
+            hand(row, place - 1, 2 - place).wait_recv()
+        keys(u)
+
+    def project_queries(row, part):
+        if (row, part) == (0, 0):
+            loads[3].wait()
+        queries(row, part)
+
     loads[0].wait()
-    hand_on(0)
+    for h in range(2):
+        hand(0, 0, h).start()
+        hand(0, 1, 1 - h).start()
     for h in range(2):
         cross(h).start()
-    loads[1].wait()
-    loads[2].wait()
-    keys(0)
-    ring(0, 0)
-    pass_on(0)
-    ring(0, 1)
-    ring(0, 2)
-    hand(0, 0, 1).wait_recv()
-    keys(1)
-    hand(0, 1, 0).wait_recv()
-    keys(2)
-    ring(0, 3)
-    ring(1, 0)
-    ring(2, 0)
-    for h in range(2):
-        cross(h).wait_recv()
-    hand_on(1)
-    ring(0, 4)
-    ring(1, 1)
-    ring(2, 1)
-    further(0, 0).wait_recv()
-    further(0, 1).wait_recv()
-    keys(3)
-    keys(4)
-    ring(1, 2)
-    ring(2, 2)
-    ring(3, 0)
-    ring(4, 0)
-    loads[3].wait()
-    queries(0, 0)
-    ring(1, 3)
-    ring(2, 3)
-    ring(3, 1)
-    ring(4, 1)
-    queries(0, 1)
-    pass_on(1)
-    ring(1, 4)
-    ring(2, 4)
-    ring(3, 2)
-    ring(4, 2)
-    hand(1, 0, 1).wait_recv()
-    keys(5)
-    hand(1, 1, 0).wait_recv()
-    keys(6)
-    ring(3, 3)
-    ring(4, 3)
-    ring(5, 0)
-    ring(6, 0)
-    further(1, 0).wait_recv()
-    further(1, 1).wait_recv()
-    keys(7)
-    ring(3, 4)
-    ring(4, 4)
-    ring(5, 1)
-    ring(6, 1)
-    ring(7, 0)
-    queries(1, 0)
-    ring(5, 2)
-    ring(6, 2)
-    ring(7, 1)
-    queries(1, 1)
-    for stage in (3, 4):
-        ring(5, stage)
-        ring(6, stage)
-        ring(7, stage - 1)
-    ring(7, 4)
+    for kind, *rest in ORDER:
+        if kind == 0:
+            pass_on(*rest[:2])
+        elif kind == 1:
+            cross_on(rest[0])
+        elif kind == 2:
+            project_keys(rest[0])
+        elif kind == 3:
+            project_queries(*rest[:2])
+        elif kind == 4:
+            ring(*rest)
+        else:
+            landed(*rest)
 
     for h in range(2):
         cross(h).wait_send()
@@ -554,9 +598,16 @@
             further(row, way).wait_send()
     for u in range(len(order)):
         y_copy(u).wait_send()
+        if u in SPLIT:
+            keep(u).wait()
         for way in range(2):
-            for hop in range(4):
-                z_copy(u, way, hop).wait_send()
+            for stage in range(4):
+                if hops(u, stage, way):
+                    z_copy(u, way, stage).wait_send()
+            if u in SPLIT:
+                for stage in range(1, 5):
+                    if hops(u, stage - 1, way):
+                        y_forward(u, stage, way).wait_send()
     done = kv_ref.at[core]
     pltpu.make_async_copy(done, done, core_send).wait()
     done = kv_ref.at[1 - core]
@@ -585,6 +636,7 @@
             dma((2, 3, 2)), dma((2, 3, 2)), dma((2, 2)), dma((2, 2)),
             dma((units,)), dma((units,)), dma((units,)),
             dma((2, 4, units)), dma((2, 4, units)),
+            dma((units, 2, 4)), dma((units, 2, 4)),
             dma, dma,
         ],
         compiler_params=pltpu.CompilerParams(collective_id=0, has_side_effects=True),

time: 146 us -> 131 us (0.90)
  Pallas kernels: 142 us -> 126 us
    pallas_call x1, Pallas kernels: 86 us -> 70.2 us  [gather(): pl.pallas_call(gather_kernel, in_specs=[hbm, hbm, hbm, hbm, vmem, vmem],...]
where the time goes in v4:
time: 131 us
  Pallas kernels  126 us (96%)
  other arithmetic  2.7 us (2%)
  local copies, waits for them, and re-layouts  1.87 us (1%)
    pallas_call x1, Pallas kernels, gather(): pl.pallas_call(gather_kernel, in_specs=[hbm, hbm, hbm, hbm, vmem, vmem],...  70.2 us
    pallas_call x1, Pallas kernels, attend(): pl.pallas_call(functools.partial(attend_kernel, n_blocks, heads), in_spec...  28.5 us
    pallas_call x1, Pallas kernels, reduce_out(): pl.pallas_call(functools.partial(reduce_kernel, shard), in_specs=[vmem, v...  27.6 us

profile of v4, /device:TPU:2, one launch (start us, length us, event | category | flops | bytes accessed | tf_op | source)
XLA Modules:
  0.0 131.0 jit_solution(5508756795150899076)
XLA Ops:
  0.0 0.7 convert_element_type.3
  0.7 1.0 fusion
  1.7 1.0 pad_maximum_fusion
  2.7 70.2 %shard_map.73 = (bf16[512,512]{1,0:T(8,128)(2,1)}, bf16[2,8,8,2,64,256]{5,4,3,2,1,0:T(8,128)(2,1)}) custom-call(bf16[64,4096]{1,0:T(8,128)(2,1)} %tokens_ref.1, bf16[4096,512]{1,0:T(8,128)(2,1)} %wq_ref.1, bf16[4096,128]{1,0:T(8,128)(2,1)} %wk_ref.1, bf16[4096,128]{1,0:T(8,128)(2,1)} %wv_ref.1, f32[512,128]{1,0:T(8,128)} %get-tuple-element.12.cos_ref, ...), custom_call_target="tpu_custom_call" | custom-call | tf_op jit(solution)/shard_map/pallas_call | solution.py:622
  72.9 28.5 %shard_map.74.mixed_ref = bf16[512,512]{1,0:T(8,128)(2,1)} custom-call(s32[4,128]{1,0:T(4,128)} %mask_ref.1, bf16[512,512]{1,0:T(8,128)(2,1)} %get-tuple-element.7.q_ref, bf16[2,8,8,2,64,256]{5,4,3,2,1,0:T(8,128)(2,1)} %get-tuple-element.8.kv_ref), custom_call_target="tpu_custom_call" | custom-call | tf_op jit(solution)/shard_map/pallas_call | solution.py:159
  101.5 27.6 %shard_map.75 = bf16[64,4096]{1,0:T(8,128)(2,1)} custom-call(bf16[512,512]{1,0:T(8,128)(2,1)} %shard_map.74.mixed_ref, bf16[512,4096]{1,0:T(8,128)(2,1)} %w_ref.1), custom_call_target="tpu_custom_call" | custom-call | tf_op jit(solution)/shard_map/pallas_call | solution.py:303
  129.1 1.9 %copy.9 = bf16[64,4096]{1,0:T(8,128)(2,1)} copy(bf16[64,4096]{1,0:T(8,128)(2,1)} %shard_map.75) | data formatting | bytes 1048576
  (1 shorter events, 0.0 us)

commit v5 on v4

--- a/solution.py
+++ b/solution.py
@@ -2,6 +2,7 @@
 
 import jax
 import jax.numpy as jnp
+import numpy as np
 from jax import lax
 from jax.experimental import pallas as pl
 from jax.experimental.pallas import tpu as pltpu
@@ -14,17 +15,12 @@
 SCALE2 = HEAD ** (-0.5) * LOG2E
 
 
-def rotary_tables(positions):
+def inverse_lanes():
     half = HEAD // 2
-    inverse = jnp.power(
-        jnp.float32(500000.0), -(2.0 * jnp.arange(half, dtype=jnp.float32)) / HEAD
-    )
-    angles = positions.astype(jnp.float32)[:, None] * inverse[None, :]
-    cosine, sine = jnp.cos(angles), jnp.sin(angles)
-    return (
-        jnp.concatenate([cosine, cosine], axis=1),
-        jnp.concatenate([-sine, sine], axis=1),
-    )
+    inverse = np.power(
+        np.float32(500000.0), -(np.float32(2.0) * np.arange(half, dtype=np.float32)) / np.float32(HEAD)
+    ).astype(np.float32)
+    return jnp.asarray(np.concatenate([inverse, inverse])[None, :])
 
 
 def turn(v, cosine, sine):
@@ -82,9 +78,8 @@
                 h * BLOCK : (h + 1) * BLOCK
             ].astype(jnp.bfloat16)
 
-    for r in range(rows):
+    def near_row(r):
         i = blk * rows + r
-        pltpu.make_async_copy(near.at[r], near.at[r], sem.at[r]).wait()
         s = score(queries(r), near[r, :, :HEAD])
         parts = [
             jnp.where(i == 1, NEG, s[:, :BLOCK]),
@@ -100,6 +95,15 @@
             p.astype(jnp.bfloat16), near[r, :, HEAD:], preferred_element_type=jnp.float32
         )
         put(r, mixed / total)
+
+    for r in range(rows):
+        pltpu.make_async_copy(near.at[r], near.at[r], sem.at[r]).wait()
+        if r:
+            near_row(r)
+
+    @pl.when(blk != 0)
+    def _():
+        near_row(0)
 
     @pl.when(blk == 0)
     def _():
@@ -195,8 +199,8 @@
 
 def reduce_kernel(
     shard, mixed_ref, w_ref, out_ref,
-    terms, far_in, near_in, pair_out, pair_in,
-    far_send, far_recv, near_send, near_recv, pair_send, pair_recv,
+    terms, far_in, near_in, pair_out, pair_in, relay_in,
+    far_send, far_recv, near_send, near_recv, pair_send, pair_recv, relay_send, relay_recv,
 ):
     at = places()
     right, left, pair = at(1, False), at(-1, False), at(0, True)
@@ -244,6 +248,21 @@
             device_id={"grp": pair}, device_id_type=MESH_ID,
         )
 
+    def relay(way):
+        return pltpu.make_async_remote_copy(
+            terms.at[RIGHT + way, 0, 1 - way], relay_in.at[way],
+            relay_send.at[way], relay_recv.at[way],
+            device_id={"grp": pair}, device_id_type=MESH_ID,
+        )
+
+    def take(way):
+        relay(way).wait_recv()
+        slot = RIGHT + way
+        terms[slot, 1, 1 - way] = (
+            terms[slot, 1, 1 - way].astype(jnp.float32) + relay_in[way].astype(jnp.float32)
+        ).astype(jnp.bfloat16)
+        near(1, way, 1 - way).start()
+
     def carry(row, way):
         far(row, way).wait_recv()
         slot = RIGHT + way
@@ -253,28 +272,27 @@
         near(row, way, way).start()
 
     def gathered(row, half):
-        near(row, 0, half).wait_recv()
-        near(row, 1, half).wait_recv()
-        return (
-            terms[OWN, row, half].astype(jnp.float32)
-            + near_in[0, row, half].astype(jnp.float32)
-            + near_in[1, row, half].astype(jnp.float32)
-        )
+        total = terms[OWN, row, half].astype(jnp.float32)
+        for way in range(2):
+            if row == 1 or way == half:
+                near(row, way, half).wait_recv()
+                total = total + near_in[way, row, half].astype(jnp.float32)
+        return total
 
     product(FAR, 2)
     far(0, 0).start()
     far(0, 1).start()
     product(RIGHT, 1)
-    near(0, 0, 1).start()
+    relay(0).start()
     product(LEFT, -1)
-    near(0, 1, 0).start()
+    relay(1).start()
     carry(0, 0)
     carry(0, 1)
     far(1, 0).start()
     far(1, 1).start()
-    near(1, 0, 1).start()
-    near(1, 1, 0).start()
     product(OWN, 0)
+    take(0)
+    take(1)
     for half in range(HALVES):
         pair_out[half] = gathered(0, half).astype(jnp.bfloat16)
         across(half).start()
@@ -289,7 +307,10 @@
         for way in range(2):
             far(row, way).wait_send()
             for half in range(HALVES):
-                near(row, way, half).wait_send()
+                if row == 1 or way == half:
+                    near(row, way, half).wait_send()
+    for way in range(2):
+        relay(way).wait_send()
     for half in range(HALVES):
         across(half).wait_send()
 
@@ -311,9 +332,11 @@
             pltpu.VMEM((2, 2, HALVES, *piece), jnp.bfloat16),
             pltpu.VMEM((HALVES, *piece), jnp.bfloat16),
             pltpu.VMEM((HALVES, *piece), jnp.bfloat16),
+            pltpu.VMEM((2, *piece), jnp.bfloat16),
             dma((2, 2)), dma((2, 2)),
             dma((2, 2, HALVES)), dma((2, 2, HALVES)),
             dma((HALVES,)), dma((HALVES,)),
+            dma((2,)), dma((2,)),
         ],
         compiler_params=pltpu.CompilerParams(collective_id=1, has_side_effects=True),
     )(mixed, w_output)
@@ -348,8 +371,8 @@
 
 
 def gather_kernel(
-    tokens_ref, wq_ref, wk_ref, wv_ref, cos_ref, sin_ref, q_ref, kv_ref,
-    tok, wq, wkv, mine,
+    tokens_ref, wq_ref, wk_ref, wv_ref, pos_ref, inv_ref, q_ref, kv_ref,
+    cos_ref, sin_ref, tok, wq, wkv, mine,
     load_sem, own_send, own_recv, far_send, far_recv,
     mine_sem, y_send, y_recv, z_send, z_recv, fwd_send, fwd_recv, core_send, core_recv,
 ):
@@ -574,6 +597,17 @@
         hand(0, 1, 1 - h).start()
     for h in range(2):
         cross(h).start()
+    lanes = lax.broadcasted_iota(jnp.int32, (1, HEAD), 1)
+    flip = jnp.where(lanes < HEAD // 2, -1.0, 1.0)
+
+    @pl.loop(0, pos_ref.shape[0])
+    def _(step):
+        here = pl.ds(pl.multiple_of(step * HEAD, HEAD), HEAD)
+        spread = jnp.broadcast_to(pos_ref[pl.ds(step, 1), :].astype(jnp.float32), (HEAD, HEAD))
+        angles = spread.T * inv_ref[...]
+        cos_ref[here, :] = jnp.cos(angles)
+        sin_ref[here, :] = jnp.sin(angles) * flip
+
     for kind, *rest in ORDER:
         if kind == 0:
             pass_on(*rest[:2])
@@ -614,7 +648,7 @@
     pltpu.make_async_copy(done, done, core_recv).wait()
 
 
-def gather(tokens, wq, wk, wv, cosine, sine, groups):
+def gather(tokens, wq, wk, wv, positions, groups):
     shard, width = tokens.shape
     units = groups
     hbm, vmem = pl.BlockSpec(memory_space=pl.ANY), pl.BlockSpec(memory_space=pltpu.VMEM)
@@ -628,6 +662,8 @@
             jax.ShapeDtypeStruct((2, Z_RING, groups, 2, shard, 2 * HEAD), jnp.bfloat16),
         ],
         scratch_shapes=[
+            pltpu.VMEM((shard * groups, HEAD), jnp.float32),
+            pltpu.VMEM((shard * groups, HEAD), jnp.float32),
             pltpu.VMEM((2, RING, shard, width), jnp.bfloat16),
             pltpu.VMEM(wq.shape, jnp.bfloat16),
             pltpu.VMEM((width, 2 * HEAD), jnp.bfloat16),
@@ -640,13 +676,12 @@
             dma, dma,
         ],
         compiler_params=pltpu.CompilerParams(collective_id=0, has_side_effects=True),
-    )(tokens, wq, wk, wv, cosine, sine)
+    )(tokens, wq, wk, wv, positions.reshape(-1, HEAD), inverse_lanes())
 
 
 def body(tokens, w_query, key_weight, value_weight, w_output, block_mask, positions):
-    cosine, sine = rotary_tables(positions)
     groups = lax.axis_size("grp")
-    q, kv = gather(tokens, w_query, key_weight, value_weight, cosine, sine, groups)
+    q, kv = gather(tokens, w_query, key_weight, value_weight, positions, groups)
     mixed = attend(block_mask, q, kv)
     return reduce_out(mixed, w_output, groups)
 

time: 131 us -> 127 us (0.969)
  other arithmetic: 2.7 us -> 0 us
where the time goes in v5:
time: 127 us
  Pallas kernels  125 us (98%)
  local copies, waits for them, and re-layouts  1.87 us (1%)
    pallas_call x1, Pallas kernels, gather(): pl.pallas_call(gather_kernel, in_specs=[hbm, hbm, hbm, hbm, vmem, vmem],...  69.9 us
    pallas_call x1, Pallas kernels, reduce_out(): pl.pallas_call(functools.partial(reduce_kernel, shard), in_specs=[vmem, v...  27.7 us
    pallas_call x1, Pallas kernels, attend(): pl.pallas_call(functools.partial(attend_kernel, n_blocks, heads), in_spec...  27.4 us

profile of v5, /device:TPU:2, one launch (start us, length us, event | category | flops | bytes accessed | tf_op | source)
XLA Modules:
  0.0 126.8 jit_solution(9707159661483479140)
XLA Ops:
  0.0 69.9 %shard_map.82 = (bf16[512,512]{1,0:T(8,128)(2,1)}, bf16[2,8,8,2,64,256]{5,4,3,2,1,0:T(8,128)(2,1)}) custom-call(bf16[64,4096]{1,0:T(8,128)(2,1)} %tokens_ref.1, bf16[4096,512]{1,0:T(8,128)(2,1)} %wq_ref.1, bf16[4096,128]{1,0:T(8,128)(2,1)} %wk_ref.1, bf16[4096,128]{1,0:T(8,128)(2,1)} %wv_ref.1, s32[4,128]{1,0:T(4,128)} %bitcast.1, ...), custom_call_target="tpu_custom_call" | custom-call | tf_op jit(solution)/shard_map/pallas_call | solution.py:656
  69.9 27.4 %shard_map.83.mixed_ref = bf16[512,512]{1,0:T(8,128)(2,1)} custom-call(s32[4,128]{1,0:T(4,128)} %mask_ref.1, bf16[512,512]{1,0:T(8,128)(2,1)} %get-tuple-element.7.q_ref, bf16[2,8,8,2,64,256]{5,4,3,2,1,0:T(8,128)(2,1)} %get-tuple-element.8.kv_ref), custom_call_target="tpu_custom_call" | custom-call | tf_op jit(solution)/shard_map/pallas_call | solution.py:163
  97.3 27.7 %shard_map.84 = bf16[64,4096]{1,0:T(8,128)(2,1)} custom-call(bf16[512,512]{1,0:T(8,128)(2,1)} %shard_map.83.mixed_ref, bf16[512,4096]{1,0:T(8,128)(2,1)} %w_ref.1), custom_call_target="tpu_custom_call" | custom-call | tf_op jit(solution)/shard_map/pallas_call | solution.py:324
  125.0 1.9 %copy.10 = bf16[64,4096]{1,0:T(8,128)(2,1)} copy(bf16[64,4096]{1,0:T(8,128)(2,1)} %shard_map.84) | data formatting | bytes 1048576

commit v6 on v5

--- a/solution.py
+++ b/solution.py
@@ -32,7 +32,7 @@
 
 
 def attend_kernel(
-    n_blocks, heads, mask_ref, q_ref, kv_ref, out_ref, near, stream, sem, stream_sem
+    n_blocks, heads, mask_ref, q_ref, kv_ref, out_ref, near, stream, ahead, sem, stream_sem
 ):
     blk = lax.axis_index("blk")
     rows = q_ref.shape[0] // BLOCK
@@ -116,35 +116,45 @@
                 stream_sem.at[slot],
             )
 
-        fetch(0, 0).start()
         q = queries(0)
         n = q.shape[0]
-
-        def body(step, state):
+        for step in range(steps):
+            fetch(step, step).start()
+
+        def keys_of(step):
+            return stream[step].reshape(-1, 2 * HEAD)
+
+        def fold(s, both, state):
             top, total, accum = state
-            slot = lax.rem(step, 2)
-            fetch(step, slot).wait()
-
-            @pl.when(step + 1 < steps)
-            def _():
-                fetch(step + 1, 1 - slot).start()
-
-            both = stream[slot].reshape(-1, 2 * HEAD)
-            s = score(q, both[:, :HEAD])
             new = jnp.maximum(top, jnp.max(s, axis=1, keepdims=True))
             p = jnp.exp2(s * SCALE2 - new * SCALE2)
             factor = jnp.exp2((top - new) * SCALE2)
             total = total * factor + jnp.sum(p, axis=1, keepdims=True)
             accum = accum * factor + jnp.dot(
-                p.astype(jnp.bfloat16),
-                both[:, HEAD:],
-                preferred_element_type=jnp.float32,
+                p.astype(jnp.bfloat16), both[:, HEAD:], preferred_element_type=jnp.float32
             )
             return new, total, accum
 
+        fetch(0, 0).wait()
+        ahead[0] = score(q, keys_of(0)[:, :HEAD])
+
+        def body(pair, state):
+            first = pair * 2
+            after = jnp.minimum(first + 2, steps - 1)
+            fetch(first + 1, first + 1).wait()
+
+            @pl.when(first + 2 < steps)
+            def _():
+                fetch(after, after).wait()
+
+            ahead[1] = score(q, keys_of(first + 1)[:, :HEAD])
+            state = fold(ahead[0], keys_of(first), state)
+            ahead[0] = score(q, keys_of(after)[:, :HEAD])
+            return fold(ahead[1], keys_of(first + 1), state)
+
         top, total, accum = lax.fori_loop(
             0,
-            steps,
+            steps // 2,
             body,
             (
                 jnp.full((n, 1), NEG, jnp.float32),
@@ -167,9 +177,10 @@
         out_shape=jax.ShapeDtypeStruct(q.shape, jnp.bfloat16),
         scratch_shapes=[
             pltpu.VMEM((rows, 7 * BLOCK, 2 * HEAD), jnp.bfloat16),
-            pltpu.VMEM((2, *kv.shape[2:]), jnp.bfloat16),
+            pltpu.VMEM((16, *kv.shape[2:]), jnp.bfloat16),
+            pltpu.VMEM((2, heads * BLOCK, 1024), jnp.float32),
             pltpu.SemaphoreType.DMA((rows,)),
-            pltpu.SemaphoreType.DMA((2,)),
+            pltpu.SemaphoreType.DMA((16,)),
         ],
     )(block_mask, q, kv)
 
@@ -195,6 +206,9 @@
     for peer in peers:
         pl.semaphore_signal(barrier, inc=1, device_id=peer, device_id_type=MESH_ID)
     pl.semaphore_wait(barrier, len(peers))
+
+
+GROUPS = 2
 
 
 def reduce_kernel(
@@ -205,11 +219,11 @@
     at = places()
     right, left, pair = at(1, False), at(-1, False), at(0, True)
     side = ({"grp": right}, {"grp": left})
-    width = w_ref.shape[1] // HALVES
+    width = w_ref.shape[1] // (GROUPS * HALVES)
     FAR, RIGHT, LEFT, OWN = 0, 1, 2, 3
     greet([side[0], side[1], {"grp": pair}])
 
-    def product(slot, dc):
+    def product(slot, dc, g):
         lhs = jnp.concatenate(
             [
                 mixed_ref[pl.ds(pl.multiple_of(at(dc, flip) * shard, shard), shard), :]
@@ -221,103 +235,115 @@
         for half in range(HALVES):
             for c in range(width // step):
                 cols = slice(c * step, (c + 1) * step)
-                wide = slice(half * width + c * step, half * width + (c + 1) * step)
-                t = jnp.dot(lhs, w_ref[:, wide], preferred_element_type=jnp.float32)
+                first = (g * HALVES + half) * width + c * step
+                t = jnp.dot(
+                    lhs, w_ref[:, first : first + step], preferred_element_type=jnp.float32
+                )
                 for row in range(2):
-                    terms[slot, row, half, :, cols] = t[
+                    terms[g, slot, row, half, :, cols] = t[
                         row * shard : (row + 1) * shard
                     ].astype(jnp.bfloat16)
 
-    def far(row, way):
-        return pltpu.make_async_remote_copy(
-            terms.at[FAR, row, way], far_in.at[way, row],
-            far_send.at[way, row], far_recv.at[way, row],
+    def far(row, way, g):
+        return pltpu.make_async_remote_copy(
+            terms.at[g, FAR, row, way], far_in.at[g, way, row],
+            far_send.at[g, way, row], far_recv.at[g, way, row],
             device_id=side[way], device_id_type=MESH_ID,
         )
 
-    def near(row, way, half):
-        return pltpu.make_async_remote_copy(
-            terms.at[RIGHT + way, row, half], near_in.at[way, row, half],
-            near_send.at[way, row, half], near_recv.at[way, row, half],
+    def near(row, way, half, g):
+        return pltpu.make_async_remote_copy(
+            terms.at[g, RIGHT + way, row, half], near_in.at[g, way, row, half],
+            near_send.at[g, way, row, half], near_recv.at[g, way, row, half],
             device_id=side[way], device_id_type=MESH_ID,
         )
 
-    def across(half):
-        return pltpu.make_async_remote_copy(
-            pair_out.at[half], pair_in.at[half], pair_send.at[half], pair_recv.at[half],
+    def across(half, g):
+        return pltpu.make_async_remote_copy(
+            pair_out.at[g, half], pair_in.at[g, half],
+            pair_send.at[g, half], pair_recv.at[g, half],
             device_id={"grp": pair}, device_id_type=MESH_ID,
         )
 
-    def relay(way):
-        return pltpu.make_async_remote_copy(
-            terms.at[RIGHT + way, 0, 1 - way], relay_in.at[way],
-            relay_send.at[way], relay_recv.at[way],
+    def relay(way, g):
+        return pltpu.make_async_remote_copy(
+            terms.at[g, RIGHT + way, 0, 1 - way], relay_in.at[g, way],
+            relay_send.at[g, way], relay_recv.at[g, way],
             device_id={"grp": pair}, device_id_type=MESH_ID,
         )
 
-    def take(way):
-        relay(way).wait_recv()
-        slot = RIGHT + way
-        terms[slot, 1, 1 - way] = (
-            terms[slot, 1, 1 - way].astype(jnp.float32) + relay_in[way].astype(jnp.float32)
+    def join(slot, row, half, g, more):
+        terms[g, slot, row, half] = (
+            terms[g, slot, row, half].astype(jnp.float32) + more.astype(jnp.float32)
         ).astype(jnp.bfloat16)
-        near(1, way, 1 - way).start()
-
-    def carry(row, way):
-        far(row, way).wait_recv()
-        slot = RIGHT + way
-        terms[slot, row, way] = (
-            terms[slot, row, way].astype(jnp.float32) + far_in[way, row].astype(jnp.float32)
-        ).astype(jnp.bfloat16)
-        near(row, way, way).start()
-
-    def gathered(row, half):
-        total = terms[OWN, row, half].astype(jnp.float32)
+
+    def take(way, g):
+        relay(way, g).wait_recv()
+        join(RIGHT + way, 1, 1 - way, g, relay_in[g, way])
+        near(1, way, 1 - way, g).start()
+
+    def carry(row, way, g):
+        far(row, way, g).wait_recv()
+        join(RIGHT + way, row, way, g, far_in[g, way, row])
+        near(row, way, way, g).start()
+
+    def gathered(row, half, g):
+        total = terms[g, OWN, row, half].astype(jnp.float32)
         for way in range(2):
             if row == 1 or way == half:
-                near(row, way, half).wait_recv()
-                total = total + near_in[way, row, half].astype(jnp.float32)
+                near(row, way, half, g).wait_recv()
+                total = total + near_in[g, way, row, half].astype(jnp.float32)
         return total
 
-    product(FAR, 2)
-    far(0, 0).start()
-    far(0, 1).start()
-    product(RIGHT, 1)
-    relay(0).start()
-    product(LEFT, -1)
-    relay(1).start()
-    carry(0, 0)
-    carry(0, 1)
-    far(1, 0).start()
-    far(1, 1).start()
-    product(OWN, 0)
-    take(0)
-    take(1)
-    for half in range(HALVES):
-        pair_out[half] = gathered(0, half).astype(jnp.bfloat16)
-        across(half).start()
-    carry(1, 0)
-    carry(1, 1)
-    for half in range(HALVES):
-        total = gathered(1, half)
-        across(half).wait_recv()
-        total = total + pair_in[half].astype(jnp.float32)
-        out_ref[:, half * width : (half + 1) * width] = total.astype(jnp.bfloat16)
-    for row in range(2):
-        for way in range(2):
-            far(row, way).wait_send()
-            for half in range(HALVES):
-                if row == 1 or way == half:
-                    near(row, way, half).wait_send()
-    for way in range(2):
-        relay(way).wait_send()
-    for half in range(HALVES):
-        across(half).wait_send()
+    groups, ways = range(GROUPS), range(2)
+    for g in groups:
+        product(FAR, 2, g)
+        for way in ways:
+            far(0, way, g).start()
+    for way in ways:
+        for g in groups:
+            product(RIGHT + way, 1 - 2 * way, g)
+            relay(way, g).start()
+    for g in groups:
+        for way in ways:
+            carry(0, way, g)
+    for g in groups:
+        for way in ways:
+            far(1, way, g).start()
+    for g in groups:
+        product(OWN, 0, g)
+    for g in groups:
+        for way in ways:
+            take(way, g)
+    for g in groups:
+        for half in range(HALVES):
+            pair_out[g, half] = gathered(0, half, g).astype(jnp.bfloat16)
+            across(half, g).start()
+    for g in groups:
+        for way in ways:
+            carry(1, way, g)
+    for g in groups:
+        for half in range(HALVES):
+            total = gathered(1, half, g)
+            across(half, g).wait_recv()
+            total = total + pair_in[g, half].astype(jnp.float32)
+            first = (g * HALVES + half) * width
+            out_ref[:, first : first + width] = total.astype(jnp.bfloat16)
+    for g in groups:
+        for way in ways:
+            for row in range(2):
+                far(row, way, g).wait_send()
+                for half in range(HALVES):
+                    if row == 1 or way == half:
+                        near(row, way, half, g).wait_send()
+            relay(way, g).wait_send()
+        for half in range(HALVES):
+            across(half, g).wait_send()
 
 
 def reduce_out(mixed, w_output, groups):
     rows, width = mixed.shape[0], w_output.shape[1]
-    shard, half = rows // groups, width // HALVES
+    shard, half = rows // groups, width // (GROUPS * HALVES)
     vmem = pl.BlockSpec(memory_space=pltpu.VMEM)
     dma = pltpu.SemaphoreType.DMA
     piece = (shard, half)
@@ -327,16 +353,16 @@
         out_specs=vmem,
         out_shape=jax.ShapeDtypeStruct((shard, width), jnp.bfloat16),
         scratch_shapes=[
-            pltpu.VMEM((4, 2, HALVES, *piece), jnp.bfloat16),
-            pltpu.VMEM((2, 2, *piece), jnp.bfloat16),
-            pltpu.VMEM((2, 2, HALVES, *piece), jnp.bfloat16),
-            pltpu.VMEM((HALVES, *piece), jnp.bfloat16),
-            pltpu.VMEM((HALVES, *piece), jnp.bfloat16),
-            pltpu.VMEM((2, *piece), jnp.bfloat16),
-            dma((2, 2)), dma((2, 2)),
-            dma((2, 2, HALVES)), dma((2, 2, HALVES)),
-            dma((HALVES,)), dma((HALVES,)),
-            dma((2,)), dma((2,)),
+            pltpu.VMEM((GROUPS, 4, 2, HALVES, *piece), jnp.bfloat16),
+            pltpu.VMEM((GROUPS, 2, 2, *piece), jnp.bfloat16),
+            pltpu.VMEM((GROUPS, 2, 2, HALVES, *piece), jnp.bfloat16),
+            pltpu.VMEM((GROUPS, HALVES, *piece), jnp.bfloat16),
+            pltpu.VMEM((GROUPS, HALVES, *piece), jnp.bfloat16),
+            pltpu.VMEM((GROUPS, 2, *piece), jnp.bfloat16),
+            dma((GROUPS, 2, 2)), dma((GROUPS, 2, 2)),
+            dma((GROUPS, 2, 2, HALVES)), dma((GROUPS, 2, 2, HALVES)),
+            dma((GROUPS, HALVES)), dma((GROUPS, HALVES)),
+            dma((GROUPS, 2)), dma((GROUPS, 2)),
         ],
         compiler_params=pltpu.CompilerParams(collective_id=1, has_side_effects=True),
     )(mixed, w_output)

time: 127 us -> 124 us (0.976)
  Pallas kernels: 125 us -> 122 us
    pallas_call x1, Pallas kernels: 27.7 us -> 25.8 us  [reduce_out(): pl.pallas_call(functools.partial(reduce_kernel, shard), in_specs=[vmem, v...]
    pallas_call x1, Pallas kernels: 27.4 us -> 25.9 us  [attend(): pl.pallas_call(functools.partial(attend_kernel, n_blocks, heads), in_spec...]
where the time goes in v6:
time: 124 us; the launch traced here: 123 us
  Pallas kernels  122 us (98%)
  local copies, waits for them, and re-layouts  1.87 us (2%)
    pallas_call x1, Pallas kernels, gather(): pl.pallas_call(gather_kernel, in_specs=[hbm, hbm, hbm, hbm, vmem, vmem],...  69.9 us
    pallas_call x1, Pallas kernels, attend(): pl.pallas_call(functools.partial(attend_kernel, n_blocks, heads), in_spec...  25.9 us
    pallas_call x1, Pallas kernels, reduce_out(): pl.pallas_call(functools.partial(reduce_kernel, shard), in_specs=[vmem, v...  25.8 us

profile of v6, /device:TPU:2, one launch (start us, length us, event | category | flops | bytes accessed | tf_op | source)
XLA Modules:
  0.0 123.4 jit_solution(8925278091904002844)
XLA Ops:
  0.0 69.9 %shard_map.82 = (bf16[512,512]{1,0:T(8,128)(2,1)}, bf16[2,8,8,2,64,256]{5,4,3,2,1,0:T(8,128)(2,1)}) custom-call(bf16[64,4096]{1,0:T(8,128)(2,1)} %tokens_ref.1, bf16[4096,512]{1,0:T(8,128)(2,1)} %wq_ref.1, bf16[4096,128]{1,0:T(8,128)(2,1)} %wk_ref.1, bf16[4096,128]{1,0:T(8,128)(2,1)} %wv_ref.1, s32[4,128]{1,0:T(4,128)} %bitcast.1, ...), custom_call_target="tpu_custom_call" | custom-call | tf_op jit(solution)/shard_map/pallas_call | solution.py:682
  69.9 25.9 %shard_map.83.mixed_ref = bf16[512,512]{1,0:T(8,128)(2,1)} custom-call(s32[4,128]{1,0:T(4,128)} %mask_ref.1, bf16[512,512]{1,0:T(8,128)(2,1)} %get-tuple-element.7.q_ref, bf16[2,8,8,2,64,256]{5,4,3,2,1,0:T(8,128)(2,1)} %get-tuple-element.8.kv_ref), custom_call_target="tpu_custom_call" | custom-call | tf_op jit(solution)/shard_map/pallas_call | solution.py:173
  95.8 25.8 %shard_map.84 = bf16[64,4096]{1,0:T(8,128)(2,1)} custom-call(bf16[512,512]{1,0:T(8,128)(2,1)} %shard_map.83.mixed_ref, bf16[512,4096]{1,0:T(8,128)(2,1)} %w_ref.1), custom_call_target="tpu_custom_call" | custom-call | tf_op jit(solution)/shard_map/pallas_call | solution.py:350
  121.6 1.9 %copy.10 = bf16[64,4096]{1,0:T(8,128)(2,1)} copy(bf16[64,4096]{1,0:T(8,128)(2,1)} %shard_map.84) | data formatting | bytes 1048576

commit v7 on v6

--- a/solution.py
+++ b/solution.py
@@ -223,15 +223,16 @@
     FAR, RIGHT, LEFT, OWN = 0, 1, 2, 3
     greet([side[0], side[1], {"grp": pair}])
 
-    def product(slot, dc, g):
+    def product(slot, dcs, g):
         lhs = jnp.concatenate(
             [
                 mixed_ref[pl.ds(pl.multiple_of(at(dc, flip) * shard, shard), shard), :]
+                for dc in dcs
                 for flip in (True, False)
             ],
             axis=0,
         )
-        step = 512
+        step = 256
         for half in range(HALVES):
             for c in range(width // step):
                 cols = slice(c * step, (c + 1) * step)
@@ -239,9 +240,9 @@
                 t = jnp.dot(
                     lhs, w_ref[:, first : first + step], preferred_element_type=jnp.float32
                 )
-                for row in range(2):
-                    terms[g, slot, row, half, :, cols] = t[
-                        row * shard : (row + 1) * shard
+                for n in range(2 * len(dcs)):
+                    terms[g, slot + n // 2, n % 2, half, :, cols] = t[
+                        n * shard : (n + 1) * shard
                     ].astype(jnp.bfloat16)
 
     def far(row, way, g):
@@ -297,12 +298,12 @@
 
     groups, ways = range(GROUPS), range(2)
     for g in groups:
-        product(FAR, 2, g)
+        product(FAR, (2,), g)
         for way in ways:
             far(0, way, g).start()
-    for way in ways:
-        for g in groups:
-            product(RIGHT + way, 1 - 2 * way, g)
+    for g in groups:
+        product(RIGHT, (1, -1, 0), g)
+        for way in ways:
             relay(way, g).start()
     for g in groups:
         for way in ways:
@@ -310,8 +311,6 @@
     for g in groups:
         for way in ways:
             far(1, way, g).start()
-    for g in groups:
-        product(OWN, 0, g)
     for g in groups:
         for way in ways:
             take(way, g)

time: 124 us -> 124 us (level)
  no operation moved by 1% of the time
where the time goes in v7:
time: 124 us; the launch traced here: 123 us
  Pallas kernels  122 us (98%)
  local copies, waits for them, and re-layouts  1.87 us (2%)
    pallas_call x1, Pallas kernels, gather(): pl.pallas_call(gather_kernel, in_specs=[hbm, hbm, hbm, hbm, vmem, vmem],...  69.9 us
    pallas_call x1, Pallas kernels, attend(): pl.pallas_call(functools.partial(attend_kernel, n_blocks, heads), in_spec...  25.9 us
    pallas_call x1, Pallas kernels, reduce_out(): pl.pallas_call(functools.partial(reduce_kernel, shard), in_specs=[vmem, v...  25.8 us

profile of v7, /device:TPU:2, one launch (start us, length us, event | category | flops | bytes accessed | tf_op | source)
XLA Modules:
  0.0 123.4 jit_solution(1406077296526038152)
XLA Ops:
  0.0 69.9 %shard_map.82 = (bf16[512,512]{1,0:T(8,128)(2,1)}, bf16[2,8,8,2,64,256]{5,4,3,2,1,0:T(8,128)(2,1)}) custom-call(bf16[64,4096]{1,0:T(8,128)(2,1)} %tokens_ref.1, bf16[4096,512]{1,0:T(8,128)(2,1)} %wq_ref.1, bf16[4096,128]{1,0:T(8,128)(2,1)} %wk_ref.1, bf16[4096,128]{1,0:T(8,128)(2,1)} %wv_ref.1, s32[4,128]{1,0:T(4,128)} %bitcast.1, ...), custom_call_target="tpu_custom_call" | custom-call | tf_op jit(solution)/shard_map/pallas_call | solution.py:681
  69.9 25.9 %shard_map.83.mixed_ref = bf16[512,512]{1,0:T(8,128)(2,1)} custom-call(s32[4,128]{1,0:T(4,128)} %mask_ref.1, bf16[512,512]{1,0:T(8,128)(2,1)} %get-tuple-element.7.q_ref, bf16[2,8,8,2,64,256]{5,4,3,2,1,0:T(8,128)(2,1)} %get-tuple-element.8.kv_ref), custom_call_target="tpu_custom_call" | custom-call | tf_op jit(solution)/shard_map/pallas_call | solution.py:173
  95.8 25.8 %shard_map.84 = bf16[64,4096]{1,0:T(8,128)(2,1)} custom-call(bf16[512,512]{1,0:T(8,128)(2,1)} %shard_map.83.mixed_ref, bf16[512,4096]{1,0:T(8,128)(2,1)} %w_ref.1), custom_call_target="tpu_custom_call" | custom-call | tf_op jit(solution)/shard_map/pallas_call | solution.py:349
  121.6 1.9 %copy.10 = bf16[64,4096]{1,0:T(8,128)(2,1)} copy(bf16[64,4096]{1,0:T(8,128)(2,1)} %shard_map.84) | data formatting | bytes 1048576
